TPU v7x, 256 devices: a whole 4x4x8 slice. The times are simulated.
256 devices in a mesh: st: 32 (over z, y), tm: 4 (over x_lo, core), pol: 2 (over x_hi).
Axes of the slice: x: 4 (x_hi: 2, x_lo: 2; x = x_hi * 2 + x_lo), y: 4, z: 8, core: 2. Of those that a mesh axis runs over, the one named last changes fastest.
Arguments:
- samples: bfloat16 [512, 262144], P('st', 'tm'), may hold values from -6 to 6
- history: bfloat16 [512, 24576], P('st'), may hold values from -6 to 6
- station_order: int32 [256], replicated, may hold values from 0 to 255, each once
- channel_order: int32 [2048], replicated, may hold values from 0 to 2047, each once
- flagged: int32 [256], replicated, may hold values 0 or 1
Outputs:
- packed: float32 [2048, 512, 512], P(('st', 'tm', 'pol'))
Inputs may be any that keep to these rules, and one draw needn't show every extreme that they name: `station_order`: each station number appears once. `channel_order`: each channel appears once.
All inputs are finite; a program needn't handle non-finite values.
Results may differ from a plain program's by a relative error of at most 0.0082.
Values may be sent and summed in bfloat16 or wider, within the bound.
A program may use at most 256 MiB of HBM per device.

v0:
```python
import math

import jax
import jax.numpy as jnp
from jax import lax
from jax.sharding import PartitionSpec as P

NFFT = 8192
FRAME_A = 32
CH = 2048
TAPS = 4


def shifted(array, axis, by):
    peers = lax.axis_size(axis)
    pairs = [(i, i + by) for i in range(peers) if 0 <= i + by < peers]
    return lax.ppermute(array, axis, pairs)


def filter_window(tap_count, frame_size):
    length = tap_count * frame_size
    offsets = jnp.arange(length).astype(jnp.float32) + 0.5
    centred = (offsets - 0.5 * length) / frame_size
    tapering = 0.5 - 0.5 * jnp.cos(offsets * (2.0 * math.pi / length))
    return (jnp.sinc(centred) * tapering).reshape(tap_count, frame_size)


def polyphase(row_block, weights, spec_count):
    row_total = row_block.shape[0]
    tap_count, frame_size = weights.shape
    running = jnp.zeros((row_total, spec_count, frame_size), jnp.float32)
    for tap_index in range(tap_count):
        section = row_block[:, tap_index * frame_size : (tap_index + spec_count) * frame_size]
        section = section.reshape(row_total, spec_count, frame_size)
        running = running + section.astype(jnp.float32) * weights[tap_index]
    return running.astype(jnp.bfloat16).reshape(row_total * spec_count, frame_size)


def trig_pair(left, right, modulus, amplitude):
    turn_count = left[:, None] * right[None, :] % modulus
    angles = turn_count.astype(jnp.float32) * (2.0 * math.pi / modulus)
    cosine = (jnp.cos(angles) * amplitude).astype(jnp.bfloat16)
    sine_part = (-(jnp.sin(angles) * amplitude)).astype(jnp.bfloat16)
    return (cosine, sine_part)


def product_low(form, left, right):
    return jnp.einsum(form, left, right, preferred_element_type=jnp.float32)


def frame_transform(filtered, channels, first_len):
    row_total, frame_size = filtered.shape
    second_len = frame_size // first_len
    half_len = second_len // 2
    first_idx = jnp.arange(first_len)
    second_idx = jnp.arange(second_len)
    half_idx = jnp.arange(half_len)
    first_cos, first_sin = trig_pair(first_idx, first_idx, first_len, 1.0 / math.sqrt(first_len))
    blocks = filtered.reshape(row_total, first_len, second_len)
    segment_re = product_low("rab,ae->reb", blocks, first_cos)
    segment_im = product_low("rab,ae->reb", blocks, first_sin)
    twist_turns = first_idx[:, None] * second_idx[None, :] % frame_size
    twist_angles = twist_turns.astype(jnp.float32) * (2.0 * math.pi / frame_size)
    twist_cos = jnp.cos(twist_angles)
    twist_sin = jnp.sin(twist_angles)
    twist_re = (segment_re * twist_cos + segment_im * twist_sin).astype(jnp.bfloat16)
    twist_im = (segment_im * twist_cos - segment_re * twist_sin).astype(jnp.bfloat16)
    second_cos, second_sin = trig_pair(
        second_idx, half_idx, second_len, 1.0 / math.sqrt(second_len)
    )
    full_re = product_low("reb,bf->ref", twist_re, second_cos) - product_low(
        "reb,bf->ref", twist_im, second_sin
    )
    full_im = product_low("reb,bf->ref", twist_re, second_sin) + product_low(
        "reb,bf->ref", twist_im, second_cos
    )
    column = channels % first_len * half_len + channels // first_len
    flat_re = jnp.take(full_re.reshape(row_total, first_len * half_len), column, axis=1)
    flat_im = jnp.take(full_im.reshape(row_total, first_len * half_len), column, axis=1)
    return jnp.stack([flat_re, flat_im], axis=1)


def input_rows(station_order):
    station_total = station_order.shape[0]
    inverse = (
        jnp.zeros((station_total,), jnp.int32).at[station_order].set(jnp.arange(station_total))
    )
    polarity = jnp.tile(jnp.arange(2), station_total)
    return 2 * jnp.repeat(inverse, 2) + polarity


def packed_products(turned, norm_scale):
    input_count, spec_count, pair_count, slot_count = turned.shape
    arranged = turned.transpose(3, 0, 1, 2)
    stacked = arranged.reshape(slot_count, input_count, spec_count * 2)
    swapped = jnp.stack([-arranged[..., 1], arranged[..., 0]], axis=-1).reshape(
        slot_count, input_count, spec_count * 2
    )
    combined = jnp.concatenate([stacked, swapped], axis=1)
    visible = jnp.einsum("sik,sjk->sij", stacked, combined, preferred_element_type=jnp.float32)
    indices = jnp.arange(input_count)
    upper_half = indices[:, None] <= indices[None, :]
    return (
        jnp.where(upper_half[None], visible[:, :, :input_count], visible[:, :, input_count:])
        * norm_scale
    )


def body(samples, history, station_order, channel_order, flagged):
    row_count, local_length = samples.shape
    spec_local = local_length // NFFT
    st_count = lax.axis_size("st")
    tm_count = lax.axis_size("tm")
    pol_count = lax.axis_size("pol")
    slot_share = CH // (st_count * tm_count * pol_count)
    half_slots = CH // pol_count
    lead_length = (TAPS - 1) * NFFT
    earlier = shifted(samples[:, local_length - lead_length :], "tm", 1)
    earlier = jnp.where(lax.axis_index("tm") == 0, history, earlier)
    stream = jnp.concatenate([earlier, samples], axis=1)
    filtered = polyphase(stream, filter_window(TAPS, NFFT), spec_local)
    local_slots = jnp.arange(half_slots)
    global_slots = (
        local_slots // slot_share * (slot_share * pol_count)
        + lax.axis_index("pol") * slot_share
        + local_slots % slot_share
    )
    station_ids = lax.dynamic_slice_in_dim(
        station_order, lax.axis_index("st") * (row_count // 2), row_count // 2
    )
    keeping = jnp.repeat((1 - flagged[station_ids]).astype(jnp.float32), 2)
    product = frame_transform(filtered, channel_order[global_slots], FRAME_A)
    product = product.reshape(row_count, spec_local, 2, half_slots) * keeping[:, None, None, None]
    spectra = product.astype(jnp.bfloat16)
    norm_scale = 1.0 / (spec_local * tm_count)
    input_order = input_rows(station_order)
    turned = lax.all_to_all(
        lax.all_to_all(spectra, "st", split_axis=3, concat_axis=0, tiled=True),
        "tm",
        split_axis=3,
        concat_axis=1,
        tiled=True,
    )
    turned = jnp.take(turned, input_order, axis=0)
    return packed_products(turned, norm_scale)


def solution(mesh):
    return jax.shard_map(
        body,
        mesh=mesh,
        in_specs=(P("st", "tm"), P("st", None), P(), P(), P()),
        out_specs=P(("st", "tm", "pol"), None, None),
        check_vma=False,
    )
```

profile of v0, /device:TPU:1, one launch (start us, length us, event | category | flops | bytes accessed | tf_op | source)
XLA Modules:
  0.0 158.4 jit_solution(5582622298725476596)
XLA Ops:
  0.0 1.2 slice.44
  1.2 4.5 %collective-permute-start = (bf16[16,24576]{1,0:T(8,128)(2,1)S(1)}, bf16[16,24576]{1,0:T(8,128)(2,1)S(1)}, u32[]{:S(2)}, u32[]{:S(2)}) collective-permute-start(bf16[16,24576]{1,0:T(8,128)(2,1)S(1)} %slice.44), channel_id=1, source_target_pairs={{0,2},{2,4},{4,6},{1,3},{3,5},{5,7},{8,10},{10,12},{12,14},{9,11},... | collective-permute-start | bytes 2359304 | tf_op jit(solution)/shard_map/ppermute | solution.py:17
  5.7 0.6 fusion.31
  6.4 3.7 %reshape.234 = f32[128,32,256]{2,1,0:T(8,128)} reshape(bf16[16,65536]{1,0:T(8,128)(2,1)} %param.7) | data formatting | bytes 6291456 | tf_op jit(solution)/shard_map/convert_element_type | solution.py:35
  10.1 0.6 gather_fusion.1
  11.0 6.2 %gather_fusion = s32[1024]{0:T(1024)S(1)} fusion(s32[2048]{0:T(1024)S(1)} %copy-done, s32[1024]{0:T(1024)S(1)} %broadcast_clamp_fusion.1), kind=kCustom, calls=%fused_computation.2 | custom fusion | bytes 12288 | tf_op jit(solution)/shard_map/gather | solution.py:132
  17.2 0.1 fusion.61
  17.5 1.3 copy-done.4
  18.7 4.6 %fusion.4 = (f32[16,65536]{1,0:T(8,128)}, f32[16,65536]{1,0:T(8,128)}, f32[16,65536]{1,0:T(8,128)}) fusion(bf16[16,65536]{1,0:T(8,128)(2,1)S(1)} %copy-done.4, bf16[16,24576]{1,0:T(8,128)(2,1)S(1)} %broadcast_select_fusion), kind=kLoop, calls=%fused_computation.18 | loop fusion | flops 12582912 | bytes 15466496 | tf_op jit(solution)/shard_map/convert_element_type | solution.py:35
  23.4 3.9 %reshape.231 = f32[128,32,256]{2,1,0:T(8,128)} reshape(f32[16,65536]{1,0:T(8,128)} %get-tuple-element.10) | data formatting | bytes 8388608 | tf_op jit(solution)/shard_map/convert_element_type | solution.py:35
  27.3 3.8 %reshape.233 = f32[128,32,256]{2,1,0:T(8,128)} reshape(f32[16,65536]{1,0:T(8,128)} %get-tuple-element.11) | data formatting | bytes 8388608 | tf_op jit(solution)/shard_map/convert_element_type | solution.py:35
  31.1 3.9 %reshape.232 = f32[128,32,256]{2,1,0:T(8,128)} reshape(f32[16,65536]{1,0:T(8,128)} %get-tuple-element.12) | data formatting | bytes 8388608 | tf_op jit(solution)/shard_map/convert_element_type | solution.py:35
  35.0 8.1 %add_convert_fusion.1 = bf16[128,32,256]{2,1,0:T(8,128)(2,1)S(1)} fusion(f32[128,32,256]{2,1,0:T(8,128)} %reshape.234, f32[128,32,256]{2,1,0:T(8,128)} %reshape.233, f32[128,32,256]{2,1,0:T(8,128)} %reshape.232, f32[128,32,256]{2,1,0:T(8,128)} %reshape.231, f32[32,256]{1,0:T(8,128)S(1)} %get-tuple-element.16, f32[32,256]{1,0:T(8,128)S(1)} %get-tuple-element.17, ...), kind=kLoop, calls=%fused_computation.10 | loop fusion | flops 8388608 | bytes 19005440 | tf_op jit(solution)/shard_map/convert_element_type | solution.py:36
  43.1 0.8 fusion.67
  43.8 1.4 fusion.5
  45.2 2.9 %fusion.8 = f32[128,32,128]{0,2,1:T(8,128)S(1)} fusion(bf16[128,32,256]{2,1,0:T(8,128)(2,1)S(1)} %get-tuple-element.9), kind=kOutput, calls=%fused_computation.25 | convolution fusion | flops 268959744 | bytes 4194304 | tf_op jit(solution)/shard_map/reb,bf->ref/dot_general | solution.py:48
  48.1 2.9 %fusion.10 = f32[128,32,128]{0,2,1:T(8,128)S(1)} fusion(bf16[128,32,256]{2,1,0:T(8,128)(2,1)S(1)} %get-tuple-element.9), kind=kOutput, calls=%fused_computation.27 | convolution fusion | flops 268992512 | bytes 4194304 | tf_op jit(solution)/shard_map/reb,bf->ref/dot_general | solution.py:48
  51.1 3.2 %fusion.16 = f32[128,32,128]{0,2,1:T(8,128)S(1)} fusion(f32[128,32,128]{0,2,1:T(8,128)S(1)} %fusion.10, bf16[128,32,256]{2,1,0:T(8,128)(2,1)S(1)} %get-tuple-element.8), kind=kOutput, calls=%fused_computation.33 | convolution fusion | flops 269484032 | bytes 6291456 | tf_op jit(solution)/shard_map/reb,bf->ref/dot_general | solution.py:48
  54.3 4.3 %fusion.19 = f32[128,32,128]{0,2,1:T(8,128)} fusion(f32[128,32,128]{0,2,1:T(8,128)S(1)} %fusion.8, bf16[128,32,256]{2,1,0:T(8,128)(2,1)S(1)} %get-tuple-element.8), kind=kOutput, calls=%fused_computation.34 | convolution fusion | flops 269516800 | bytes 6291456 | tf_op jit(solution)/shard_map/reb,bf->ref/dot_general | solution.py:48
  58.7 4.4 %gather_fusion.4 = f32[1024,128]{1,0:T(8,128)S(1)} fusion(f32[128,4096]{0,1:T(8,128)} %bitcast.51, s32[1024]{0:T(1024)S(1)} %broadcast_clamp_fusion), kind=kCustom, calls=%fused_computation.1.clone | custom fusion | bytes 1052672 | tf_op jit(solution)/shard_map/jit(_take)/gather | solution.py:79
  63.1 2.8 %gather_fusion.3 = f32[1024,128]{1,0:T(8,128)S(1)} fusion(f32[128,4096]{0,1:T(8,128)S(1)} %bitcast.50, s32[1024]{0:T(1024)S(1)} %broadcast_clamp_fusion), kind=kCustom, calls=%fused_computation.clone | custom fusion | bytes 1052672 | tf_op jit(solution)/shard_map/jit(_take)/gather | solution.py:78
  65.9 0.2 select_bitcast_fusion.2
  66.1 0.2 copy.56
  66.3 0.2 copy.59
  66.6 4.8 %copy.60 = bf16[16,8,2,1024]{0,1,2,3:T(8,128)(2,1)} copy(bf16[16,8,2,1024]{3,1,0,2:T(8,128)(2,1)S(1)} %fusion.22) | data formatting | bytes 1048576 | tf_op jit(solution)/shard_map/convert_element_type | solution.py:134
  71.4 7.1 %reshape.297 = bf16[32,2,4096]{2,1,0:T(2,128)(2,1)} reshape(bf16[1024,2,8,16]{3,2,1,0:T(8,128)(2,1)} %bitcast.52) | data formatting | bytes 1048576
  78.5 11.2 %all-to-all-start = ((bf16[32,2,4096]{2,1,0:T(2,128)(2,1)}), bf16[32,2,4096]{2,1,0:T(2,128)(2,1)S(1)}, u32[]{:S(2)}, u32[]{:S(2)}) async-start(bf16[32,2,4096]{2,1,0:T(2,128)(2,1)} %reshape.297), calls=%async_computation | async-start | bytes 1048576 | tf_op jit(solution)/shard_map/all_to_all | solution.py:138
  89.7 1.4 scatter_custom_fusion
  91.3 0.1 add.364
  91.4 15.4 %all-to-all-done = bf16[32,2,4096]{2,1,0:T(2,128)(2,1)S(1)} async-done(((bf16[32,2,4096]{2,1,0:T(2,128)(2,1)}), bf16[32,2,4096]{2,1,0:T(2,128)(2,1)S(1)}, u32[]{:S(2)}, u32[]{:S(2)}) %all-to-all-start) | async-done | bytes 524320 | tf_op jit(solution)/shard_map/all_to_all | solution.py:138
  106.8 4.1 %reshape.298 = bf16[1024,2,8,16]{3,2,1,0:T(8,128)(2,1)} reshape(bf16[32,2,4096]{2,1,0:T(2,128)(2,1)S(1)} %all-to-all-done) | data formatting | bytes 1048576
  110.8 5.7 %copy.61 = bf16[16,8,2,32,32]{4,1,2,0,3:T(8,128)(2,1)S(1)} copy(bf16[16,8,2,32,32]{0,1,2,4,3:T(8,128)(2,1)} %bitcast.53) | data formatting | bytes 1048576 | tf_op jit(solution)/shard_map/all_to_all | solution.py:138
  116.5 2.9 %copy.62 = bf16[512,8,2,32]{0,1,2,3:T(8,128)(2,1)} copy(bf16[512,8,2,32]{3,1,2,0:T(8,128)(2,1)S(1)} %bitcast.54) | data formatting | bytes 1048576 | tf_op jit(solution)/shard_map/all_to_all | solution.py:138
  119.4 3.7 %all-to-all-start.1 = ((bf16[512,8,2,32]{0,1,2,3:T(8,128)(2,1)}), bf16[512,8,2,32]{0,1,2,3:T(8,128)(2,1)S(1)}, u32[]{:S(2)}, u32[]{:S(2)}) async-start(bf16[512,8,2,32]{0,1,2,3:T(8,128)(2,1)} %copy.62), calls=%async_computation.1 | async-start | bytes 1048576 | tf_op jit(solution)/shard_map/all_to_all | solution.py:137
  123.1 0.1 add.329
  123.4 7.6 %all-to-all-done.1 = bf16[512,8,2,32]{0,1,2,3:T(8,128)(2,1)S(1)} async-done(((bf16[512,8,2,32]{0,1,2,3:T(8,128)(2,1)}), bf16[512,8,2,32]{0,1,2,3:T(8,128)(2,1)S(1)}, u32[]{:S(2)}, u32[]{:S(2)}) %all-to-all-start.1) | async-done | bytes 524320 | tf_op jit(solution)/shard_map/all_to_all | solution.py:137
  131.0 0.3 copy.64
  131.3 3.0 %copy.65 = bf16[512,32,2,8]{1,3,2,0:T(8,128)(2,1)} copy(bf16[512,32,2,8]{0,3,2,1:T(8,128)(2,1)S(1)} %bitcast.55) | data formatting | bytes 1048576 | tf_op jit(solution)/shard_map/all_to_all | solution.py:137
  134.3 2.8 %gather_fusion.2 = bf16[512,32,2,8]{1,3,2,0:T(8,128)(2,1)S(1)} fusion(bf16[512,32,2,8]{1,3,2,0:T(8,128)(2,1)} %copy.65, s32[1024]{0:T(1024)S(1)} %pad_clamp_fusion), kind=kCustom, calls=%fused_computation.4 | custom fusion | bytes 1050624 | tf_op jit(solution)/shard_map/jit(_take)/gather | solution.py:144
  137.1 2.6 %select_bitcast_fusion = bf16[8,512,32,2]{2,0,3,1:T(8,128)(2,1)} fusion(bf16[512,32,2,8]{1,3,2,0:T(8,128)(2,1)S(1)} %gather_fusion.2, pred[512]{0:T(512)(128)(4,1)S(1)} %compare_and_fusion.1), kind=kLoop, calls=%fused_computation.24 | loop fusion | flops 262144 | bytes 1049088 | tf_op jit(solution)/shard_map/jit(_take)/select_n | solution.py:144
  139.7 4.5 %copy.66 = bf16[8,512,32,2]{1,3,2,0:T(2,128)(2,1)} copy(bf16[8,512,32,2]{2,0,3,1:T(8,128)(2,1)} %select_bitcast_fusion) | data formatting | bytes 1048576 | tf_op jit(solution)/shard_map/jit(_take)/select_n | solution.py:144
  144.2 1.2 slice_negate_fusion
  145.4 2.0 %reshape.229 = bf16[8,512,64]{1,2,0:T(8,128)(2,1)} reshape(bf16[8,512,32,2]{1,3,2,0:T(2,128)(2,1)} %copy.66) | data formatting | bytes 1048576 | tf_op jit(solution)/shard_map/reshape | solution.py:95
  147.5 1.7 %pad_maximum_fusion.1 = bf16[8,512,32,2]{2,0,3,1:T(8,128)(2,1)S(1)} fusion(bf16[8,512,32,1]{2,0,3,1:T(8,128)(2,1)} %get-tuple-element.14, bf16[8,512,32,1]{2,0,3,1:T(8,128)(2,1)S(1)} %get-tuple-element.13), kind=kLoop, calls=%fused_computation.23 | loop fusion | flops 262144 | bytes 1048576 | tf_op jit(solution)/shard_map/stack | solution.py:96
  149.2 2.1 %copy.67 = bf16[8,512,32,2]{1,3,2,0:T(2,128)(2,1)S(1)} copy(bf16[8,512,32,2]{2,0,3,1:T(8,128)(2,1)S(1)} %pad_maximum_fusion.1) | data formatting | bytes 1048576 | tf_op jit(solution)/shard_map/stack | solution.py:96
  151.3 0.2 reshape.230
  151.5 2.4 %fusion.23 = f32[8,512,1024]{2,1,0:T(8,128)S(1)} fusion(bf16[8,512,64]{1,2,0:T(8,128)(2,1)S(1)} %copy-done.5, bf16[8,512,64]{1,2,0:T(8,128)(2,1)S(1)} %reshape.230), kind=kOutput, calls=%fused_computation.38 | convolution fusion | flops 538968064 | bytes 17825792 | tf_op jit(solution)/shard_map/sik,sjk->sij/dot_general | solution.py:100
  153.9 4.5 %fusion = f32[8,512,512]{2,1,0:T(8,128)} fusion(f32[8,512,1024]{2,1,0:T(8,128)S(1)} %fusion.23, pred[512,512]{1,0:T(8,128)(4,1)S(1)} %iota_compare_fusion), kind=kLoop, calls=%fused_computation.7 | loop fusion | flops 4194304 | bytes 25427968 | tf_op jit(solution)/shard_map/mul | solution.py:104
  (36 shorter events, 0.8 us)
Async XLA Ops:
  0.0 11.0 %copy-start = (s32[2048]{0:T(1024)S(1)}, s32[2048]{0:T(1024)}, u32[]{:S(2)}) copy-start(s32[2048]{0:T(1024)} %param.10) | copy-start | bytes 24580
  1.2 16.2 %collective-permute-start = (bf16[16,24576]{1,0:T(8,128)(2,1)S(1)}, bf16[16,24576]{1,0:T(8,128)(2,1)S(1)}, u32[]{:S(2)}, u32[]{:S(2)}) collective-permute-start(bf16[16,24576]{1,0:T(8,128)(2,1)S(1)} %slice.44), channel_id=1, source_target_pairs={{0,2},{2,4},{4,6},{1,3},{3,5},{5,7},{8,10},{10,12},{12,14},{9,11},... | collective-permute-start | bytes 2359304 | tf_op jit(solution)/shard_map/ppermute | solution.py:17
  6.3 3.7 %copy-start.7 = (s32[256]{0:T(256)S(1)}, s32[256]{0:T(256)}, u32[]{:S(2)}) copy-start(s32[256]{0:T(256)} %param.9) | copy-start | bytes 3076
  6.4 3.8 %copy-start.2 = (s32[256]{0:T(256)S(1)}, s32[256]{0:T(256)}, u32[]{:S(2)}) copy-start(s32[256]{0:T(256)} %param.11) | copy-start | bytes 3076
  11.0 6.4 %copy-start.6 = (bf16[16,24576]{1,0:T(8,128)(2,1)S(1)}, bf16[16,24576]{1,0:T(8,128)(2,1)}, u32[]{:S(2)}) copy-start(bf16[16,24576]{1,0:T(8,128)(2,1)} %param.8) | copy-start | bytes 2359300
  17.1 1.6 %copy-start.4 = (bf16[16,65536]{1,0:T(8,128)(2,1)S(1)}, bf16[16,65536]{1,0:T(8,128)(2,1)}, u32[]{:S(2)}) copy-start(bf16[16,65536]{1,0:T(8,128)(2,1)} %param.7) | copy-start | bytes 6291460
  78.5 28.3 %all-to-all-start = ((bf16[32,2,4096]{2,1,0:T(2,128)(2,1)}), bf16[32,2,4096]{2,1,0:T(2,128)(2,1)S(1)}, u32[]{:S(2)}, u32[]{:S(2)}) async-start(bf16[32,2,4096]{2,1,0:T(2,128)(2,1)} %reshape.297), calls=%async_computation | async-start | bytes 1048576 | tf_op jit(solution)/shard_map/all_to_all | solution.py:138
  119.4 11.6 %all-to-all-start.1 = ((bf16[512,8,2,32]{0,1,2,3:T(8,128)(2,1)}), bf16[512,8,2,32]{0,1,2,3:T(8,128)(2,1)S(1)}, u32[]{:S(2)}, u32[]{:S(2)}) async-start(bf16[512,8,2,32]{0,1,2,3:T(8,128)(2,1)} %copy.62), calls=%async_computation.1 | async-start | bytes 1048576 | tf_op jit(solution)/shard_map/all_to_all | solution.py:137
  139.7 4.5 %copy-start.3 = (bf16[8,512,32,2]{2,0,3,1:T(8,128)(2,1)S(1)}, bf16[8,512,32,2]{2,0,3,1:T(8,128)(2,1)}, u32[]{:S(2)}) copy-start(bf16[8,512,32,2]{2,0,3,1:T(8,128)(2,1)} %select_bitcast_fusion) | copy-start | bytes 1572868
  149.2 2.3 %copy-start.5 = (bf16[8,512,64]{1,2,0:T(8,128)(2,1)S(1)}, bf16[8,512,64]{1,2,0:T(8,128)(2,1)}, u32[]{:S(2)}) copy-start(bf16[8,512,64]{1,2,0:T(8,128)(2,1)} %reshape.229) | copy-start | bytes 1572868
  153.9 4.5 %copy-start.1 = (s32[2048]{0:T(1024)S(1)}, s32[2048]{0:T(1024)}, u32[]{:S(2)}) copy-start(s32[2048]{0:T(1024)} %param.10) | copy-start | bytes 24580
where the time goes:
time: 159 us; the launch traced here: 158 us
  local copies, waits for them, and re-layouts  73.4 us (46%)
  other arithmetic  24.3 us (15%)
  waiting for transfers between devices  23 us (14%)
  starting transfers between devices  19.4 us (12%)
  matrix products  17.9 us (11%)
    dot_general x6, matrix products, product_low(): return jnp.einsum(form, left, right, preferred_element_type=jnp.float32)  15.5 us
    all_to_all x1, waiting for transfers between devices, body(): lax.all_to_all(spectra, 'st', split_axis=3, concat_axis=0, tiled=True)  15.4 us
    convert_element_type x4, local copies, waits for them, and re-layouts, polyphase(): running = running + section.astype(jnp.float32) * weights[tap_index]  15.2 us
    unnamed x18, local copies, waits for them, and re-layouts  12.4 us
    all_to_all x1, starting transfers between devices, body(): lax.all_to_all(spectra, 'st', split_axis=3, concat_axis=0, tiled=True)  11.2 us
    all_to_all x2, local copies, waits for them, and re-layouts, body(): lax.all_to_all(spectra, 'st', split_axis=3, concat_axis=0, tiled=True)  8.53 us
    convert_element_type x1, other arithmetic, polyphase(): running.astype(jnp.bfloat16).reshape(row_total * spec_count, frame_size)  8.1 us
    all_to_all x1, waiting for transfers between devices, body(): lax.all_to_all(lax.all_to_all(spectra, 'st', split_axis=3, concat_axis=0,...  7.64 us
  transfers between devices with their start and end apart: 3, of which 2 were waited for; matrix products, arithmetic and copies ran while one was open for 8% of the time, Pallas kernels for 0%

commit v1 on v0

v1 whole, which is shorter than its diff:
```python
import functools
import math

import jax
import jax.numpy as jnp
import numpy as np
from jax import lax
from jax.experimental import pallas as pl
from jax.experimental.pallas import tpu as pltpu
from jax.sharding import PartitionSpec as P

import ml_dtypes

NFFT = 8192
FRAME_A = 32
FRAME_B = NFFT // FRAME_A
CH = 2048
TAPS = 4
LEAD = TAPS - 1
ROWS = 8
FRAMES = 8
PEERS = 256
MESH = pl.DeviceIdType.MESH
Z_OFFSETS = (1, 7, 2, 6, 3, 5, 4, 0)
BF16 = jnp.bfloat16
F32 = jnp.float32


def constants():
    bf = ml_dtypes.bfloat16
    length = TAPS * NFFT
    m = np.arange(length) + 0.5
    window = np.sinc((m - 0.5 * length) / NFFT) * (0.5 - 0.5 * np.cos(m * (2.0 * math.pi / length)))
    window = window.reshape(TAPS, NFFT).astype(np.float32)
    a = np.arange(FRAME_A)
    angle = (a[:, None] * a[None, :] % FRAME_A) * (2.0 * math.pi / FRAME_A)
    cos = np.cos(angle) / math.sqrt(FRAME_A)
    sin = -np.sin(angle) / math.sqrt(FRAME_A)
    first = np.concatenate([cos[:, :17], sin[:, 1:16]], axis=1).T.astype(bf)
    first = np.kron(first.astype(np.float32), np.eye(ROWS, dtype=np.float32)).astype(bf)
    b = np.arange(FRAME_B)
    twist = (a[:, None] * b[None, :] % NFFT) * (2.0 * math.pi / NFFT)
    twist_cos = np.repeat(np.cos(twist), ROWS, axis=0).astype(np.float32)
    twist_sin = np.repeat(np.sin(twist), ROWS, axis=0).astype(np.float32)
    f = np.arange(CH // FRAME_A)
    angle = (b[:, None] * f[None, :] % FRAME_B) * (2.0 * math.pi / FRAME_B)
    cos = (np.cos(angle) / math.sqrt(FRAME_B)).astype(bf)
    sin = (-np.sin(angle) / math.sqrt(FRAME_B)).astype(bf)
    second = np.concatenate([np.concatenate([cos, sin], 1), np.concatenate([-sin, cos], 1)], 0)
    t, p, f = np.meshgrid(np.arange(FRAMES), np.arange(2), np.arange(64), indexing="ij")
    perm = np.zeros((1024, 1024), np.float32)
    perm[(t * 128 + p * 64 + f).ravel(), (f * 16 + p * 8 + t).ravel()] = 1
    return window, first, twist_cos, twist_sin, second, perm.astype(bf)


def filterbank_kernel(
    place, samples, halo, window_h, first_h, tcos_h, tsin_h, second_h, perm_h, keep, out,
    stream, window, first, tcos, tsin, second, perm, filtered, lanes, full, sem,
):
    rows = pl.ds(pl.multiple_of(lax.axis_index("pol") * ROWS, ROWS), ROWS)
    lead = LEAD * NFFT
    moves = [
        (samples.at[rows], stream.at[:, pl.ds(lead, FRAMES * NFFT)]),
        (halo, stream.at[:, pl.ds(0, lead)]),
        (window_h, window), (first_h, first), (tcos_h, tcos), (tsin_h, tsin),
        (second_h, second), (perm_h, perm),
    ]
    copies = [pltpu.make_async_copy(s, d, sem.at[i]) for i, (s, d) in enumerate(moves)]
    for c in copies:
        c.start()
    for c in copies[:3]:
        c.wait()

    def taps(i, carry):
        parts = []
        for half in range(2):
            off = i // 2 * 512 + half * 256 + i % 2 * 128
            w = [
                jnp.broadcast_to(window[k : k + 1, pl.ds(pl.multiple_of(off, 128), 128)], (ROWS, 128))
                for k in range(TAPS)
            ]
            x = [
                stream[:, pl.ds(pl.multiple_of(off + j * NFFT, 128), 128)].astype(F32)
                for j in range(FRAMES + LEAD)
            ]
            parts.append([sum(w[k] * x[t + k] for k in range(TAPS)) for t in range(FRAMES)])
        for t in range(FRAMES):
            block = jnp.concatenate([parts[0][t], parts[1][t]], axis=0).astype(BF16)
            filtered[t, pl.ds(pl.multiple_of(i // 2 * 16, 16), 16), pl.ds(pl.multiple_of(i % 2 * 128, 128), 128)] = block
        return carry

    lax.fori_loop(0, 32, taps, 0)
    for c in copies[3:7]:
        c.wait()

    def frame(t, carry):
        seg = jnp.dot(first[...], filtered[t], preferred_element_type=F32)
        res, ims = [], []
        for e in range(FRAME_A):
            s = min(e, FRAME_A - e)
            rs = slice(e * ROWS, (e + 1) * ROWS)
            c, n = tcos[rs, :], tsin[rs, :]
            re = seg[s * ROWS : (s + 1) * ROWS]
            if s in (0, 16):
                res.append(re * c)
                ims.append(-(re * n))
            else:
                im = seg[(16 + s) * ROWS : (17 + s) * ROWS]
                if e < 16:
                    res.append(re * c + im * n)
                    ims.append(im * c - re * n)
                else:
                    res.append(re * c - im * n)
                    ims.append(-(im * c) - re * n)
        tw = jnp.concatenate(
            [jnp.concatenate(res, axis=0).astype(BF16), jnp.concatenate(ims, axis=0).astype(BF16)], axis=1
        )
        spec = jnp.dot(tw, second[...], preferred_element_type=F32) * keep[...]
        lanes[:, pl.ds(pl.multiple_of(t * 128, 128), 128)] = spec.astype(BF16)
        return carry

    lax.fori_loop(0, FRAMES, frame, 0)
    copies[7].wait()
    for q in range(4):
        turned = jnp.dot(lanes[...], perm[:, q * 256 : (q + 1) * 256], preferred_element_type=F32)
        for h in range(2):
            block = 2 * q + h
            full[block * 32 : (block + 1) * 32] = turned[:, h * 128 : (h + 1) * 128].reshape(32, ROWS, 128)

    lane = lax.broadcasted_iota(jnp.int32, (ROWS, 128), 1) // 16

    def gather(d, carry):
        acc = None
        for j in range(8):
            g = d * 8 + j
            v = pltpu.roll(full[place[0, g]], place[1, g], 1)
            acc = v if acc is None else jnp.where(lane == j, v, acc)
        out[d] = acc.astype(BF16)
        return carry

    lax.fori_loop(0, PEERS, gather, 0, unroll=2)


def filterbank(place, samples, halo, keep):
    consts = [jnp.asarray(c) for c in constants()]
    anyspec = pl.BlockSpec(memory_space=pl.ANY)
    vmem = pl.BlockSpec(memory_space=pltpu.VMEM)
    return pl.pallas_call(
        filterbank_kernel,
        out_shape=jax.ShapeDtypeStruct((PEERS, 8, 128), BF16),
        in_specs=[pl.BlockSpec(memory_space=pltpu.SMEM)] + [anyspec] * 8 + [vmem],
        out_specs=vmem,
        scratch_shapes=[
            pltpu.VMEM((ROWS, (FRAMES + LEAD) * NFFT), BF16),
            pltpu.VMEM((TAPS, NFFT), F32),
            pltpu.VMEM((256, 256), BF16),
            pltpu.VMEM((256, 256), F32),
            pltpu.VMEM((256, 256), F32),
            pltpu.VMEM((512, 128), BF16),
            pltpu.VMEM((1024, 1024), BF16),
            pltpu.VMEM((FRAMES, 256, 256), BF16),
            pltpu.VMEM((256, 1024), BF16),
            pltpu.VMEM((256, ROWS, 128), F32),
            pltpu.SemaphoreType.DMA((8,)),
        ],
        compiler_params=pltpu.CompilerParams(vmem_limit_bytes=40 << 20),
        name="filterbank",
    )(place, samples, halo, *consts, keep)


def exchange_kernel(src, dst, send_sem, recv_sem, own_sem):
    st, tm, pol = lax.axis_index("st"), lax.axis_index("tm"), lax.axis_index("pol")
    z, y, w = st // 4, st % 4, tm * 2 + pol
    zs = [(z + o) % 8 for o in Z_OFFSETS]

    def each(action):
        def step(o, carry):
            yy, ww = (y + o % 4) % 4, (w + o // 4) % 8
            for j in range(8):
                s = zs[j] * 4 + yy
                if Z_OFFSETS[j]:
                    action(s, ww // 2, ww % 2)
                else:
                    pl.when(o != 0)(lambda s=s: action(s, ww // 2, ww % 2))
            return carry

        lax.fori_loop(0, 32, step, 0)

    barrier = pltpu.get_barrier_semaphore()
    each(lambda a, b, c: pl.semaphore_signal(barrier, inc=1, device_id=(a, b, c), device_id_type=MESH))
    pl.semaphore_wait(barrier, PEERS - 1)
    slot = st * 2 + pol

    def send(a, b, c):
        pltpu.make_async_remote_copy(
            src.at[a * 8 + b * 2 + c], dst.at[tm * 64 + slot], send_sem, recv_sem,
            device_id=(a, b, c), device_id_type=MESH,
        ).start()

    each(send)
    own = pltpu.make_async_copy(src.at[st * 8 + w], dst.at[tm * 64 + slot], own_sem)
    own.start()
    own.wait()
    part = pl.ds(0, PEERS - 1)
    pltpu.make_async_copy(src.at[part], dst.at[part], send_sem).wait()
    pltpu.make_async_copy(src.at[part], dst.at[part], recv_sem).wait()


def exchange(messages):
    vmem = pl.BlockSpec(memory_space=pltpu.VMEM)
    return pl.pallas_call(
        exchange_kernel,
        out_shape=jax.ShapeDtypeStruct((PEERS, 8, 128), BF16),
        in_specs=[vmem],
        out_specs=vmem,
        scratch_shapes=[pltpu.SemaphoreType.DMA] * 3,
        compiler_params=pltpu.CompilerParams(collective_id=0, has_side_effects=True),
        name="exchange",
    )(messages)


def correlate_kernel(turned, target, out, parts, swapped):
    slot = pl.program_id(0)

    @pl.when(slot == 0)
    def _():
        inputs = lax.broadcasted_iota(jnp.int32, (512, 512), 1)
        onehot = (target[...] == inputs).astype(F32).astype(BF16)
        for tm in range(4):
            got = lax.dot_general(
                turned[tm], onehot, (((0,), (0,)), ((), ())), preferred_element_type=F32
            )
            for s in range(8):
                re, im = got[16 * s : 16 * s + 8], got[16 * s + 8 : 16 * s + 16]
                parts[s, 16 * tm : 16 * tm + 16] = jnp.concatenate([re, im], axis=0).astype(BF16)
                swapped[s, 16 * tm : 16 * tm + 16] = jnp.concatenate([-im, re], axis=0).astype(BF16)

    part, swap = parts[slot], swapped[slot]

    def product(i, right, j):
        return lax.dot_general(
            part[:, i * 256 : i * 256 + 256], right[:, j * 256 : j * 256 + 256],
            (((0,), (0,)), ((), ())), preferred_element_type=F32,
        )

    upper = lax.broadcasted_iota(jnp.int32, (256, 256), 0) <= lax.broadcasted_iota(jnp.int32, (256, 256), 1)
    for i in range(2):
        for j in range(2):
            if i == j:
                block = jnp.where(upper, product(i, part, j), product(i, swap, j))
            else:
                block = product(i, part if i < j else swap, j)
            out[0, i * 256 : i * 256 + 256, j * 256 : j * 256 + 256] = block * (1.0 / 32)


def correlate(turned, target):
    return pl.pallas_call(
        correlate_kernel,
        out_shape=jax.ShapeDtypeStruct((8, 512, 512), F32),
        grid=(8,),
        in_specs=[
            pl.BlockSpec((4, 512, 128), lambda s: (0, 0, 0)),
            pl.BlockSpec((512, 1), lambda s: (0, 0)),
        ],
        out_specs=pl.BlockSpec((1, 512, 512), lambda s: (s, 0, 0)),
        scratch_shapes=[pltpu.VMEM((8, 64, 512), BF16), pltpu.VMEM((8, 64, 512), BF16)],
        compiler_params=pltpu.CompilerParams(vmem_limit_bytes=24 << 20),
        name="correlate",
    )(turned, target)


def body(samples, history, station_order, channel_order, flagged):
    tm, pol = lax.axis_index("tm"), lax.axis_index("pol")
    length = samples.shape[1]
    lead = LEAD * NFFT
    first_row = pol * ROWS
    tail = lax.dynamic_slice(samples, (first_row, length - lead), (ROWS, lead))
    earlier = lax.ppermute(tail, "tm", [(i, i + 1) for i in range(3)])
    own = lax.dynamic_slice(history, (first_row, 0), (ROWS, lead))
    halo = jnp.where(tm == 0, own, earlier)
    f = channel_order // FRAME_A
    slots = jnp.arange(CH) % 8
    place = jnp.stack([f // 8 * 32 + channel_order % FRAME_A, (slots - f % 8) * 16 % 128])
    stations = lax.dynamic_slice_in_dim(station_order, lax.axis_index("st") * 8 + pol * 4, 4)
    keep = jnp.repeat(1 - flagged[stations], 2).astype(F32)
    keep = jnp.tile(keep[None], (FRAME_A, 1)).reshape(FRAME_A * ROWS, 1)
    messages = filterbank(place, samples, halo, keep)
    turned = exchange(messages).reshape(4, 512, 128)
    target = (2 * station_order[:, None] + jnp.arange(2)[None]).reshape(512, 1)
    return correlate(turned, target)


def solution(mesh):
    return jax.shard_map(
        body,
        mesh=mesh,
        in_specs=(P("st", "tm"), P("st", None), P(), P(), P()),
        out_specs=P(("st", "tm", "pol"), None, None),
        check_vma=False,
    )
```

time: 159 us -> 76.4 us (0.48)
  local copies, waits for them, and re-layouts: 73.4 us -> 6.37 us
  Pallas kernels: 0 us -> 59.8 us
  waiting for transfers between devices: 23 us -> 1.67 us
  other arithmetic: 24.3 us -> 3.5 us
  matrix products: 17.9 us -> 0 us
  starting transfers between devices: 19.4 us -> 4.5 us
    pallas_call x0 -> x3, Pallas kernels: none -> 59.8 us  [the longest x1 32.2 us: exchange(): pl.pallas_call(exchange_kernel, out_shape=jax.ShapeDtypeStruct((PEERS, 8,...]
    all_to_all x2 -> x0, waiting for transfers between devices: 23 us -> none  [the longest x1 15.4 us: body(): lax.all_to_all(spectra, 'st', split_axis=3, concat_axis=0, tiled=True)]
    convert_element_type x5 -> x1, local copies, waits for them, and re-layouts: 20.1 us -> 0.09 us  [body(): keep = jnp.repeat(1 - flagged[stations], 2).astype(F32)]
    dot_general x7 -> x0, matrix products: 17.9 us -> none  [the longest x6 15.5 us: product_low(): return jnp.einsum(form, left, right, preferred_element_type=jnp.float32)]
    gather x5 -> x1, local copies, waits for them, and re-layouts: 16.8 us -> 0.64 us  [body(): keep = jnp.repeat(1 - flagged[stations], 2).astype(F32)]
    all_to_all x2 -> x0, starting transfers between devices: 14.9 us -> none  [the longest x1 11.2 us: body(): lax.all_to_all(spectra, 'st', split_axis=3, concat_axis=0, tiled=True)]
    convert_element_type x4 -> x1, other arithmetic: 12.9 us -> 0.01 us  [body(): keep = jnp.repeat(1 - flagged[stations], 2).astype(F32)]
    all_to_all x4 -> x0, local copies, waits for them, and re-layouts: 11.8 us -> none  [the longest x2 8.53 us: body(): lax.all_to_all(spectra, 'st', split_axis=3, concat_axis=0, tiled=True)]
  transfers between devices with their start and end apart: 3 -> 1, of which waited for: 2 -> 1; matrix products, arithmetic and copies ran while one was open for 8% -> 4% of each run, Pallas kernels for 0% -> 0%
where the time goes in v1:
time: 76.4 us; the launch traced here: 76.1 us
  Pallas kernels  59.8 us (78%)
  local copies, waits for them, and re-layouts  6.37 us (8%)
  starting transfers between devices  4.5 us (6%)
  other arithmetic  3.5 us (5%)
  waiting for transfers between devices  1.67 us (2%)
    pallas_call x1, Pallas kernels, exchange(): pl.pallas_call(exchange_kernel, out_shape=jax.ShapeDtypeStruct((PEERS, 8,...  32.2 us
    pallas_call x1, Pallas kernels, filterbank(): pl.pallas_call(filterbank_kernel, out_shape=jax.ShapeDtypeStruct((PEERS,...  21.2 us
    pallas_call x1, Pallas kernels, correlate(): pl.pallas_call(correlate_kernel, out_shape=jax.ShapeDtypeStruct((8, 512,...  6.4 us
    ppermute x1, starting transfers between devices, body(): earlier = lax.ppermute(tail, 'tm', [(i, i + 1) for i in range(3)])  4.5 us
    unnamed x20, local copies, waits for them, and re-layouts  3.45 us
    dynamic_slice x1, local copies, waits for them, and re-layouts, body(): tail = lax.dynamic_slice(samples, (first_row, length - lead), (ROWS, lead))  1.92 us
    ppermute x1, waiting for transfers between devices, body(): earlier = lax.ppermute(tail, 'tm', [(i, i + 1) for i in range(3)])  1.67 us
  transfers between devices with their start and end apart: 1, of which 1 were waited for; matrix products, arithmetic and copies ran while one was open for 4% of the time, Pallas kernels for 0%

profile of v1, /device:TPU:1, one launch (start us, length us, event | category | flops | bytes accessed | tf_op | source)
XLA Modules:
  0.0 76.1 jit_solution(3060459014418665570)
XLA Ops:
  0.0 0.0 copy-start
  0.0 0.0 copy-start.7
  0.0 0.0 copy-start.5
  0.0 0.0 copy-start.6
  0.0 0.0 copy-start.8
  0.0 0.0 copy-start.9
  0.1 0.0 copy-start.1
  0.1 1.9 %constant_dynamic-slice_fusion = bf16[8,24576]{1,0:T(8,128)(2,1)} fusion(bf16[16,65536]{1,0:T(8,128)(2,1)} %samples.1, s32[]{:T(128)S(6)} %select_n.52), kind=kLoop, calls=%fused_computation.37 | loop fusion | bytes 786436 | tf_op jit(solution)/shard_map/dynamic_slice | solution.py:277
  2.0 4.5 %collective-permute-start = (bf16[8,24576]{1,0:T(8,128)(2,1)}, bf16[8,24576]{1,0:T(8,128)(2,1)}, u32[]{:S(2)}, u32[]{:S(2)}) collective-permute-start(bf16[8,24576]{1,0:T(8,128)(2,1)} %constant_dynamic-slice_fusion), channel_id=1, source_target_pairs={{0,2},{2,4},{4,6},{1,3},{3,5},{5,7},{8,10},{10,12},{12,14},{9,11},... | collective-permute-start | bytes 1179656 | tf_op jit(solution)/shard_map/ppermute | solution.py:278
  6.5 0.7 broadcast_multiply_fusion
  7.2 0.8 compare_select_fusion
  8.0 0.0 copy-done
  8.0 0.6 gather_fusion
  8.6 0.1 broadcast_in_dim.9
  8.7 0.1 convert_element_type.12
  8.8 0.1 reshape_tile.4.keep
  8.9 0.1 iota_add_fusion
  9.0 0.1 add.72.target
  9.1 0.7 fusion.1
  9.8 1.7 %collective-permute-done = bf16[8,24576]{1,0:T(8,128)(2,1)} collective-permute-done((bf16[8,24576]{1,0:T(8,128)(2,1)}, bf16[8,24576]{1,0:T(8,128)(2,1)}, u32[]{:S(2)}, u32[]{:S(2)}) %collective-permute-start) | collective-permute-done | bytes 393248 | tf_op jit(solution)/shard_map/ppermute | solution.py:278
  11.5 1.2 %dynamic-slice_select_fusion.halo = bf16[8,24576]{1,0:T(8,128)(2,1)S(1)} fusion(bf16[8,24576]{1,0:T(8,128)(2,1)} %collective-permute-done, bf16[16,24576]{1,0:T(8,128)(2,1)} %param.12, s32[]{:T(128)S(6)} %select_n.52, pred[]{:T(512)S(6)} %eq.8), kind=kLoop, calls=%fused_computation.1 | loop fusion | flops 196608 | bytes 1179653 | tf_op jit(solution)/shard_map/jit(_where)/select_n | solution.py:280
  12.7 0.0 copy-done.7
  12.7 0.0 copy-done.5
  12.7 0.0 copy-done.6
  12.8 0.0 copy-done.8
  12.8 0.0 copy-done.9
  12.8 0.0 copy-done.1
  12.8 0.0 copy-start.2
  12.8 1.6 %copy-done.2 = bf16[1024,1024]{1,0:T(8,128)(2,1)S(1)} copy-done((bf16[1024,1024]{1,0:T(8,128)(2,1)S(1)}, bf16[1024,1024]{1,0:T(8,128)(2,1)}, u32[]{:S(2)}) %copy-start.2) | copy-done | bytes 2097176
  14.4 21.2 %filterbank.1.src = bf16[256,8,128]{2,1,0:T(8,128)(2,1)S(1)} custom-call(s32[2,2048]{1,0:T(2,128)S(1)} %pad_add_fusion.place, bf16[16,65536]{1,0:T(8,128)(2,1)S(1)} %copy-done.1, bf16[8,24576]{1,0:T(8,128)(2,1)S(1)} %dynamic-slice_select_fusion.halo, f32[4,8192]{1,0:T(4,128)S(1)} %copy-done.9, bf16[256,256]{1,0:T(8,128)(2,1)S(1)} %copy-done.8, ...), custom_call_target="tpu_custom_call" | custom-call | tf_op jit(solution)/shard_map/filterbank/pallas_call | solution.py:148
  35.6 0.0 copy-start.3
  35.6 0.8 %copy-done.3 = bf16[256,8,128]{2,1,0:T(8,128)(2,1)} copy-done((bf16[256,8,128]{2,1,0:T(8,128)(2,1)}, bf16[256,8,128]{2,1,0:T(8,128)(2,1)S(1)}, u32[]{:S(2)}) %copy-start.3) | copy-done | bytes 524312
  36.4 32.2 %exchange.1 = bf16[256,8,128]{2,1,0:T(8,128)(2,1)} custom-call(bf16[256,8,128]{2,1,0:T(8,128)(2,1)} %copy-done.3), custom_call_target="tpu_custom_call" | custom-call | tf_op jit(solution)/shard_map/exchange/pallas_call | solution.py:211
  68.6 0.0 copy-start.4
  68.6 1.0 %copy-done.4 = bf16[256,8,128]{2,1,0:T(8,128)(2,1)S(1)} copy-done((bf16[256,8,128]{2,1,0:T(8,128)(2,1)S(1)}, bf16[256,8,128]{2,1,0:T(8,128)(2,1)}, u32[]{:S(2)}) %copy-start.4) | copy-done | bytes 524312
  69.7 6.4 %correlate.1 = f32[8,512,512]{2,1,0:T(8,128)} custom-call(bf16[4,512,128]{2,1,0:T(8,128)(2,1)S(1)} %bitcast.7, s32[512,1]{1,0:T(8,128)S(1)} %add.72.target), custom_call_target="tpu_custom_call" | custom-call | tf_op jit(solution)/shard_map/correlate/pallas_call | solution.py:257
  (4 shorter events, 0.0 us)
Async XLA Ops:
  0.0 8.0 %copy-start = (s32[256]{0:T(256)S(1)}, s32[256]{0:T(256)}, u32[]{:S(2)}) copy-start(s32[256]{0:T(256)} %param.15) | copy-start | bytes 3076
  0.0 12.7 %copy-start.7 = (bf16[512,128]{1,0:T(8,128)(2,1)S(1)}, bf16[512,128]{1,0:T(8,128)(2,1)}, u32[]{:S(2)}) copy-start(bf16[512,128]{1,0:T(8,128)(2,1)} %constant.110.clone.second_h) | copy-start | bytes 393220
  0.0 12.7 %copy-start.5 = (f32[256,256]{1,0:T(8,128)S(1)}, f32[256,256]{1,0:T(8,128)}, u32[]{:S(2)}) copy-start(f32[256,256]{1,0:T(8,128)} %constant.109.clone.tsin_h) | copy-start | bytes 786436
  0.0 12.7 %copy-start.6 = (f32[256,256]{1,0:T(8,128)S(1)}, f32[256,256]{1,0:T(8,128)}, u32[]{:S(2)}) copy-start(f32[256,256]{1,0:T(8,128)} %constant.108.clone.tcos_h) | copy-start | bytes 786436
  0.0 12.7 %copy-start.8 = (bf16[256,256]{1,0:T(8,128)(2,1)S(1)}, bf16[256,256]{1,0:T(8,128)(2,1)}, u32[]{:S(2)}) copy-start(bf16[256,256]{1,0:T(8,128)(2,1)} %constant.107.clone.first_h) | copy-start | bytes 393220
  0.0 12.7 %copy-start.9 = (f32[4,8192]{1,0:T(4,128)S(1)}, f32[4,8192]{1,0:T(4,128)}, u32[]{:S(2)}) copy-start(f32[4,8192]{1,0:T(4,128)} %constant.106.clone.window_h) | copy-start | bytes 393220
  0.1 12.7 %copy-start.1 = (bf16[16,65536]{1,0:T(8,128)(2,1)S(1)}, bf16[16,65536]{1,0:T(8,128)(2,1)}, u32[]{:S(2)}) copy-start(bf16[16,65536]{1,0:T(8,128)(2,1)} %samples.1) | copy-start | bytes 6291460
  2.0 9.5 %collective-permute-start = (bf16[8,24576]{1,0:T(8,128)(2,1)}, bf16[8,24576]{1,0:T(8,128)(2,1)}, u32[]{:S(2)}, u32[]{:S(2)}) collective-permute-start(bf16[8,24576]{1,0:T(8,128)(2,1)} %constant_dynamic-slice_fusion), channel_id=1, source_target_pairs={{0,2},{2,4},{4,6},{1,3},{3,5},{5,7},{8,10},{10,12},{12,14},{9,11},... | collective-permute-start | bytes 1179656 | tf_op jit(solution)/shard_map/ppermute | solution.py:278
  12.8 1.6 %copy-start.2 = (bf16[1024,1024]{1,0:T(8,128)(2,1)S(1)}, bf16[1024,1024]{1,0:T(8,128)(2,1)}, u32[]{:S(2)}) copy-start(bf16[1024,1024]{1,0:T(8,128)(2,1)} %constant.111.clone.perm_h) | copy-start | bytes 6291460
  35.6 0.8 %copy-start.3 = (bf16[256,8,128]{2,1,0:T(8,128)(2,1)}, bf16[256,8,128]{2,1,0:T(8,128)(2,1)S(1)}, u32[]{:S(2)}) copy-start(bf16[256,8,128]{2,1,0:T(8,128)(2,1)S(1)} %filterbank.1.src) | copy-start | bytes 1572868
  68.6 1.0 %copy-start.4 = (bf16[256,8,128]{2,1,0:T(8,128)(2,1)S(1)}, bf16[256,8,128]{2,1,0:T(8,128)(2,1)}, u32[]{:S(2)}) copy-start(bf16[256,8,128]{2,1,0:T(8,128)(2,1)} %exchange.1) | copy-start | bytes 1572868

commit v2 on v1

v2 whole, which is shorter than its diff:
```python
import functools
import math

import jax
import jax.numpy as jnp
import numpy as np
from jax import lax
from jax.experimental import pallas as pl
from jax.experimental.pallas import tpu as pltpu
from jax.sharding import PartitionSpec as P

import ml_dtypes

NFFT = 8192
FRAME_A = 32
FRAME_B = NFFT // FRAME_A
CH = 2048
TAPS = 4
LEAD = TAPS - 1
ROWS = 8
FRAMES = 8
PEERS = 256
MESH = pl.DeviceIdType.MESH
Z_OFFSETS = (1, 7, 2, 6, 3, 5, 4, 0)
BF16 = jnp.bfloat16
F32 = jnp.float32


def constants():
    bf = ml_dtypes.bfloat16
    length = TAPS * NFFT
    m = np.arange(length) + 0.5
    window = np.sinc((m - 0.5 * length) / NFFT) * (0.5 - 0.5 * np.cos(m * (2.0 * math.pi / length)))
    window = window.reshape(TAPS, NFFT).astype(np.float32)
    a = np.arange(FRAME_A)
    angle = (a[:, None] * a[None, :] % FRAME_A) * (2.0 * math.pi / FRAME_A)
    cos = np.cos(angle) / math.sqrt(FRAME_A)
    sin = -np.sin(angle) / math.sqrt(FRAME_A)
    first = np.concatenate([cos[:, :17], sin[:, 1:16]], axis=1).T.astype(bf)
    first = np.kron(first.astype(np.float32), np.eye(ROWS, dtype=np.float32)).astype(bf)
    b = np.arange(FRAME_B)
    twist = (a[:, None] * b[None, :] % NFFT) * (2.0 * math.pi / NFFT)
    twist_cos = np.repeat(np.cos(twist), ROWS, axis=0).astype(np.float32)
    twist_sin = np.repeat(np.sin(twist), ROWS, axis=0).astype(np.float32)
    f = np.arange(CH // FRAME_A)
    angle = (b[:, None] * f[None, :] % FRAME_B) * (2.0 * math.pi / FRAME_B)
    cos = (np.cos(angle) / math.sqrt(FRAME_B)).astype(bf)
    sin = (-np.sin(angle) / math.sqrt(FRAME_B)).astype(bf)
    second = np.concatenate([np.concatenate([cos, sin], 1), np.concatenate([-sin, cos], 1)], 0)
    t, p, f = np.meshgrid(np.arange(FRAMES), np.arange(2), np.arange(64), indexing="ij")
    perm = np.zeros((1024, 1024), np.float32)
    perm[(t * 128 + p * 64 + f).ravel(), (f * 16 + p * 8 + t).ravel()] = 1
    return window, first, twist_cos, twist_sin, second, perm.astype(bf)


def spectra_kernel(
    channels, stations, flags, samples, history, window_h, first_h, tcos_h, tsin_h, second_h, perm_h, out, onehot,
    stream, window, first, tcos, tsin, second, perm, filtered, lanes, full, messages,
    sem, lead_sem, lead_send, send_sem, recv_sem, own_sem,
):
    st, tm, pol = lax.axis_index("st"), lax.axis_index("tm"), lax.axis_index("pol")
    z, y, w = st // 4, st % 4, tm * 2 + pol
    zs = [(z + o) % 8 for o in Z_OFFSETS]

    def each(action, o):
        yy, ww = (y + o % 4) % 4, (w + o // 4) % 8
        for j in range(8):
            action(j, zs[j] * 4 + yy, ww // 2, ww % 2)

    def when_other(j, o, action):
        if Z_OFFSETS[j]:
            action()
        else:
            pl.when(o != 0)(action)

    lead = LEAD * NFFT
    half = lead // 2
    rows = pl.ds(pl.multiple_of(pol * ROWS, ROWS), ROWS)
    moves = [
        (samples.at[rows], stream.at[:, pl.ds(lead, FRAMES * NFFT)]),
        (window_h, window), (first_h, first), (tcos_h, tcos), (tsin_h, tsin),
        (second_h, second), (perm_h, perm),
    ]
    copies = [pltpu.make_async_copy(s, d, sem.at[i]) for i, (s, d) in enumerate(moves)]
    for c in copies:
        c.start()
    before = pltpu.make_async_copy(history.at[rows], stream.at[:, pl.ds(0, lead)], sem.at[7])
    pl.when(tm == 0)(before.start)

    barrier = pltpu.get_barrier_semaphore()

    def greet(o, carry):
        def signal(j, a, b, c):
            when_other(j, o, lambda: pl.semaphore_signal(
                barrier, inc=1, device_id=(a, b, c), device_id_type=MESH
            ))

        each(signal, o)
        return carry

    lax.fori_loop(0, 32, greet, 0)
    for c in copies[:2]:
        c.wait()

    def taps(lo, hi):
        def step(i, carry):
            parts = []
            for h in range(2):
                off = i // 2 * 512 + h * 256 + i % 2 * 128
                w = [
                    jnp.broadcast_to(window[k : k + 1, pl.ds(pl.multiple_of(off, 128), 128)], (ROWS, 128))
                    for k in range(TAPS)
                ]
                x = {
                    j: stream[:, pl.ds(pl.multiple_of(off + j * NFFT, 128), 128)].astype(F32)
                    for j in range(lo, hi + LEAD)
                }
                parts.append([sum(w[k] * x[t + k] for k in range(TAPS)) for t in range(lo, hi)])
            for t in range(lo, hi):
                block = jnp.concatenate([parts[0][t - lo], parts[1][t - lo]], axis=0).astype(BF16)
                filtered[
                    t, pl.ds(pl.multiple_of(i // 2 * 16, 16), 16), pl.ds(pl.multiple_of(i % 2 * 128, 128), 128)
                ] = block
            return carry

        lax.fori_loop(0, 32, step, 0)

    row = lax.broadcasted_iota(jnp.int32, (ROWS, 128), 0) // 2
    keep = jnp.zeros((ROWS, 128), F32)
    for i in range(ROWS // 2):
        flag = 1 - flags[stations[st * 8 + pol * 4 + i]]
        keep = jnp.where(row == i, flag.astype(F32), keep)
    keep = jnp.tile(keep, (FRAME_A, 1))

    def frame(t, carry):
        seg = jnp.dot(first[...], filtered[t], preferred_element_type=F32)
        res, ims = [], []
        for e in range(FRAME_A):
            s = min(e, FRAME_A - e)
            rs = slice(e * ROWS, (e + 1) * ROWS)
            c, n = tcos[rs, :], tsin[rs, :]
            re = seg[s * ROWS : (s + 1) * ROWS]
            if s in (0, 16):
                res.append(re * c)
                ims.append(-(re * n))
            else:
                im = seg[(16 + s) * ROWS : (17 + s) * ROWS]
                if e < 16:
                    res.append(re * c + im * n)
                    ims.append(im * c - re * n)
                else:
                    res.append(re * c - im * n)
                    ims.append(-(im * c) - re * n)
        tw = jnp.concatenate(
            [jnp.concatenate(res, axis=0).astype(BF16), jnp.concatenate(ims, axis=0).astype(BF16)], axis=1
        )
        spec = jnp.dot(tw, second[...], preferred_element_type=F32) * keep
        lanes[:, pl.ds(pl.multiple_of(t * 128, 128), 128)] = spec.astype(BF16)
        return carry

    taps(LEAD, FRAMES)
    for c in copies[2:6]:
        c.wait()
    lax.fori_loop(LEAD, FRAMES, frame, 0)

    pl.semaphore_wait(barrier, PEERS - 1)

    def lead_copy(i, b, c):
        src = samples.at[
            pl.ds(pl.multiple_of(c * ROWS, ROWS), ROWS), pl.ds(FRAMES * NFFT - lead + i * half, half)
        ]
        return pltpu.make_async_remote_copy(
            src, stream.at[:, pl.ds(i * half, half)], lead_send.at[i], lead_sem.at[i],
            device_id=(st, b, c), device_id_type=MESH,
        )

    after = (tm + 1) % 4
    across = (pol + after + 1) % 2
    leads = [lead_copy(0, after, pol), lead_copy(1, after, across)]

    @pl.when(tm != 3)
    def _():
        for c in leads:
            c.start()

    @pl.when(tm != 0)
    def _():
        for c in leads:
            c.wait_recv()

    pl.when(tm == 0)(before.wait)
    taps(0, LEAD)
    lax.fori_loop(0, LEAD, frame, 0)
    copies[6].wait()
    for q in range(4):
        turned = jnp.dot(lanes[...], perm[:, q * 256 : (q + 1) * 256], preferred_element_type=F32)
        for h in range(2):
            block = 2 * q + h
            full[block * 32 : (block + 1) * 32] = turned[:, h * 128 : (h + 1) * 128].reshape(32, ROWS, 128)

    lane = lax.broadcasted_iota(jnp.int32, (ROWS, 128), 1) // 16
    slot = tm * 64 + st * 2 + pol

    def send(o, carry):
        def one(j, a, b, c):
            peer = a * 8 + b * 2 + c
            acc = None
            for i in range(8):
                ch = channels[peer * 8 + i]
                v = full[ch // 256 * 32 + ch % 32]
                v = pltpu.roll(v, (8 + i - ch // 32 % 8) % 8 * 16, 1)
                acc = v if acc is None else jnp.where(lane == i, v, acc)
            messages[peer] = acc.astype(BF16)
            when_other(j, o, pltpu.make_async_remote_copy(
                messages.at[peer], out.at[slot], send_sem, recv_sem,
                device_id=(a, b, c), device_id_type=MESH,
            ).start)

        each(one, o)
        return carry

    lax.fori_loop(0, 32, send, 0)
    own = pltpu.make_async_copy(messages.at[st * 8 + w], out.at[slot], own_sem)
    own.start()

    inputs = lax.broadcasted_iota(jnp.int32, (16, 512), 1)
    pair = lax.broadcasted_iota(jnp.int32, (16, 512), 0)

    def target(i, carry):
        at = jnp.zeros((16, 512), jnp.int32)
        for p in range(8):
            at = jnp.where(pair // 2 == p, 2 * stations[i * 8 + p], at)
        onehot[pl.ds(pl.multiple_of(i * 16, 16), 16), :] = (at + pair % 2 == inputs).astype(F32).astype(BF16)
        return carry

    lax.fori_loop(0, 32, target, 0)

    @pl.when(tm != 3)
    def _():
        for c in leads:
            c.wait_send()

    own.wait()
    part = pl.ds(0, PEERS - 1)
    pltpu.make_async_copy(messages.at[part], out.at[part], send_sem).wait()
    pltpu.make_async_copy(messages.at[part], out.at[part], recv_sem).wait()


def spectra(channels, stations, flags, samples, history):
    consts = [jnp.asarray(c) for c in constants()]
    anyspec = pl.BlockSpec(memory_space=pl.ANY)
    vmem = pl.BlockSpec(memory_space=pltpu.VMEM)
    smem = pl.BlockSpec(memory_space=pltpu.SMEM)
    return pl.pallas_call(
        spectra_kernel,
        out_shape=[jax.ShapeDtypeStruct((PEERS, ROWS, 128), BF16), jax.ShapeDtypeStruct((512, 512), BF16)],
        in_specs=[smem] * 3 + [anyspec] * 8,
        out_specs=[vmem, vmem],
        scratch_shapes=[
            pltpu.VMEM((ROWS, (FRAMES + LEAD) * NFFT), BF16),
            pltpu.VMEM((TAPS, NFFT), F32),
            pltpu.VMEM((256, 256), BF16),
            pltpu.VMEM((256, 256), F32),
            pltpu.VMEM((256, 256), F32),
            pltpu.VMEM((512, 128), BF16),
            pltpu.VMEM((1024, 1024), BF16),
            pltpu.VMEM((FRAMES, 256, 256), BF16),
            pltpu.VMEM((256, 1024), BF16),
            pltpu.VMEM((256, ROWS, 128), F32),
            pltpu.VMEM((PEERS, ROWS, 128), BF16),
            pltpu.SemaphoreType.DMA((8,)),
            pltpu.SemaphoreType.DMA((2,)),
            pltpu.SemaphoreType.DMA((2,)),
        ] + [pltpu.SemaphoreType.DMA] * 3,
        compiler_params=pltpu.CompilerParams(
            vmem_limit_bytes=40 << 20, collective_id=0, has_side_effects=True
        ),
        name="spectra",
    )(channels, stations, flags, samples, history, *consts)


def correlate_kernel(turned, onehot, out, parts, swapped):
    slot = pl.program_id(0)

    @pl.when(slot == 0)
    def _():
        for tm in range(4):
            got = lax.dot_general(
                turned[tm], onehot[...], (((0,), (0,)), ((), ())), preferred_element_type=F32
            )
            for s in range(8):
                re, im = got[16 * s : 16 * s + 8], got[16 * s + 8 : 16 * s + 16]
                parts[s, 16 * tm : 16 * tm + 16] = jnp.concatenate([re, im], axis=0).astype(BF16)
                swapped[s, 16 * tm : 16 * tm + 16] = jnp.concatenate([-im, re], axis=0).astype(BF16)

    part, swap = parts[slot], swapped[slot]

    def product(i, right, j):
        return lax.dot_general(
            part[:, i * 256 : i * 256 + 256], right[:, j * 256 : j * 256 + 256],
            (((0,), (0,)), ((), ())), preferred_element_type=F32,
        )

    upper = lax.broadcasted_iota(jnp.int32, (256, 256), 0) <= lax.broadcasted_iota(jnp.int32, (256, 256), 1)
    for i in range(2):
        for j in range(2):
            if i == j:
                block = jnp.where(upper, product(i, part, j), product(i, swap, j))
            else:
                block = product(i, part if i < j else swap, j)
            out[0, i * 256 : i * 256 + 256, j * 256 : j * 256 + 256] = block * (1.0 / 32)


def correlate(turned, onehot):
    return pl.pallas_call(
        correlate_kernel,
        out_shape=jax.ShapeDtypeStruct((8, 512, 512), F32),
        grid=(8,),
        in_specs=[
            pl.BlockSpec((4, 512, 128), lambda s: (0, 0, 0)),
            pl.BlockSpec((512, 512), lambda s: (0, 0)),
        ],
        out_specs=pl.BlockSpec((1, 512, 512), lambda s: (s, 0, 0)),
        scratch_shapes=[pltpu.VMEM((8, 64, 512), BF16), pltpu.VMEM((8, 64, 512), BF16)],
        compiler_params=pltpu.CompilerParams(vmem_limit_bytes=24 << 20),
        name="correlate",
    )(turned, onehot)


def body(samples, history, station_order, channel_order, flagged):
    turned, onehot = spectra(channel_order, station_order, flagged, samples, history)
    return correlate(turned.reshape(4, 512, 128), onehot)


def solution(mesh):
    return jax.shard_map(
        body,
        mesh=mesh,
        in_specs=(P("st", "tm"), P("st", None), P(), P(), P()),
        out_specs=P(("st", "tm", "pol"), None, None),
        check_vma=False,
    )
```

time: 76.4 us -> 82.4 us (1.079)
  the two profiles are of different devices: /device:TPU:1 before, /device:TPU:2 now
where the time goes in v2:
time: 82.4 us; the launch traced here: 82 us
  Pallas kernels  71 us (86%)
  local copies, waits for them, and re-layouts  11 us (13%)
    pallas_call x1, Pallas kernels, spectra(): pl.pallas_call(spectra_kernel, out_shape=[jax.ShapeDtypeStruct((PEERS, RO...  64.7 us
    unnamed x22, local copies, waits for them, and re-layouts  11 us
    pallas_call x1, Pallas kernels, correlate(): pl.pallas_call(correlate_kernel, out_shape=jax.ShapeDtypeStruct((8, 512,...  6.33 us

profile of v2, /device:TPU:2, one launch (start us, length us, event | category | flops | bytes accessed | tf_op | source)
XLA Modules:
  0.0 82.0 jit_solution(10564251645432731255)
XLA Ops:
  0.0 0.0 copy-start
  0.0 1.6 %copy-done = bf16[16,65536]{1,0:T(8,128)(2,1)S(1)} copy-done((bf16[16,65536]{1,0:T(8,128)(2,1)S(1)}, bf16[16,65536]{1,0:T(8,128)(2,1)}, u32[]{:S(2)}) %copy-start) | copy-done | bytes 2097176
  1.6 0.0 copy-start.1
  1.6 1.6 %copy-done.1 = bf16[1024,1024]{1,0:T(8,128)(2,1)S(1)} copy-done((bf16[1024,1024]{1,0:T(8,128)(2,1)S(1)}, bf16[1024,1024]{1,0:T(8,128)(2,1)}, u32[]{:S(2)}) %copy-start.1) | copy-done | bytes 2097176
  3.2 0.0 copy-start.2
  3.2 1.1 %copy-done.2 = bf16[16,24576]{1,0:T(8,128)(2,1)S(1)} copy-done((bf16[16,24576]{1,0:T(8,128)(2,1)S(1)}, bf16[16,24576]{1,0:T(8,128)(2,1)}, u32[]{:S(2)}) %copy-start.2) | copy-done | bytes 786456
  4.3 0.0 copy-start.3
  4.3 0.9 %copy-done.3 = f32[256,256]{1,0:T(8,128)S(1)} copy-done((f32[256,256]{1,0:T(8,128)S(1)}, f32[256,256]{1,0:T(8,128)}, u32[]{:S(2)}) %copy-start.3) | copy-done | bytes 262168
  5.3 0.0 copy-start.4
  5.3 0.9 %copy-done.4 = f32[256,256]{1,0:T(8,128)S(1)} copy-done((f32[256,256]{1,0:T(8,128)S(1)}, f32[256,256]{1,0:T(8,128)}, u32[]{:S(2)}) %copy-start.4) | copy-done | bytes 262168
  6.2 0.0 copy-start.5
  6.2 0.9 %copy-done.5 = bf16[512,128]{1,0:T(8,128)(2,1)S(1)} copy-done((bf16[512,128]{1,0:T(8,128)(2,1)S(1)}, bf16[512,128]{1,0:T(8,128)(2,1)}, u32[]{:S(2)}) %copy-start.5) | copy-done | bytes 131096
  7.1 0.0 copy-start.6
  7.1 0.9 %copy-done.6 = bf16[256,256]{1,0:T(8,128)(2,1)S(1)} copy-done((bf16[256,256]{1,0:T(8,128)(2,1)S(1)}, bf16[256,256]{1,0:T(8,128)(2,1)}, u32[]{:S(2)}) %copy-start.6) | copy-done | bytes 131096
  8.0 0.0 copy-start.7
  8.0 0.9 %copy-done.7 = f32[4,8192]{1,0:T(4,128)S(1)} copy-done((f32[4,8192]{1,0:T(4,128)S(1)}, f32[4,8192]{1,0:T(4,128)}, u32[]{:S(2)}) %copy-start.7) | copy-done | bytes 131096
  8.9 0.0 copy-start.8
  8.9 0.7 copy-done.8
  9.6 0.0 copy-start.9
  9.6 0.7 copy-done.9
  10.3 0.0 copy-start.10
  10.3 0.7 copy-done.10
  11.0 64.7 %spectra.1 = (bf16[256,8,128]{2,1,0:T(8,128)(2,1)S(1)}, bf16[512,512]{1,0:T(8,128)(2,1)S(1)}) custom-call(s32[2048]{0:T(1024)S(1)} %copy-done.8, s32[256]{0:T(256)S(1)} %copy-done.9, s32[256]{0:T(256)S(1)} %copy-done.10, bf16[16,65536]{1,0:T(8,128)(2,1)S(1)} %copy-done, bf16[16,24576]{1,0:T(8,128)(2,1)S(1)} %copy-done.2, f32[4,8192]{1,0:T(4,128)S(1)} %copy-done.7, ...), custom_call_target="tpu_custom_call" | custom-call | tf_op jit(solution)/shard_map/spectra/pallas_call | solution.py:254
  75.7 6.3 %correlate.1 = f32[8,512,512]{2,1,0:T(8,128)} custom-call(bf16[4,512,128]{2,1,0:T(8,128)(2,1)S(1)} %bitcast.1, bf16[512,512]{1,0:T(8,128)(2,1)S(1)} %get-tuple-element.8.onehot), custom_call_target="tpu_custom_call" | custom-call | tf_op jit(solution)/shard_map/correlate/pallas_call | solution.py:315
Async XLA Ops:
  0.0 1.6 %copy-start = (bf16[16,65536]{1,0:T(8,128)(2,1)S(1)}, bf16[16,65536]{1,0:T(8,128)(2,1)}, u32[]{:S(2)}) copy-start(bf16[16,65536]{1,0:T(8,128)(2,1)} %samples.1) | copy-start | bytes 6291460
  1.6 1.6 %copy-start.1 = (bf16[1024,1024]{1,0:T(8,128)(2,1)S(1)}, bf16[1024,1024]{1,0:T(8,128)(2,1)}, u32[]{:S(2)}) copy-start(bf16[1024,1024]{1,0:T(8,128)(2,1)} %constant.17.clone.perm_h) | copy-start | bytes 6291460
  3.2 1.1 %copy-start.2 = (bf16[16,24576]{1,0:T(8,128)(2,1)S(1)}, bf16[16,24576]{1,0:T(8,128)(2,1)}, u32[]{:S(2)}) copy-start(bf16[16,24576]{1,0:T(8,128)(2,1)} %history.1) | copy-start | bytes 2359300
  4.3 0.9 %copy-start.3 = (f32[256,256]{1,0:T(8,128)S(1)}, f32[256,256]{1,0:T(8,128)}, u32[]{:S(2)}) copy-start(f32[256,256]{1,0:T(8,128)} %constant.15.clone.tsin_h) | copy-start | bytes 786436
  5.3 0.9 %copy-start.4 = (f32[256,256]{1,0:T(8,128)S(1)}, f32[256,256]{1,0:T(8,128)}, u32[]{:S(2)}) copy-start(f32[256,256]{1,0:T(8,128)} %constant.14.clone.tcos_h) | copy-start | bytes 786436
  6.2 0.9 %copy-start.5 = (bf16[512,128]{1,0:T(8,128)(2,1)S(1)}, bf16[512,128]{1,0:T(8,128)(2,1)}, u32[]{:S(2)}) copy-start(bf16[512,128]{1,0:T(8,128)(2,1)} %constant.16.clone.second_h) | copy-start | bytes 393220
  7.1 0.9 %copy-start.6 = (bf16[256,256]{1,0:T(8,128)(2,1)S(1)}, bf16[256,256]{1,0:T(8,128)(2,1)}, u32[]{:S(2)}) copy-start(bf16[256,256]{1,0:T(8,128)(2,1)} %constant.13.clone.first_h) | copy-start | bytes 393220
  8.0 0.9 %copy-start.7 = (f32[4,8192]{1,0:T(4,128)S(1)}, f32[4,8192]{1,0:T(4,128)}, u32[]{:S(2)}) copy-start(f32[4,8192]{1,0:T(4,128)} %constant.12.clone.window_h) | copy-start | bytes 393220
  8.9 0.7 copy-start.8
  9.6 0.7 copy-start.9
  10.3 0.7 copy-start.10

commit v3 on v2

--- a/solution.py
+++ b/solution.py
@@ -54,9 +54,9 @@
 
 
 def spectra_kernel(
-    channels, stations, flags, samples, history, window_h, first_h, tcos_h, tsin_h, second_h, perm_h, out, onehot,
+    channels_h, stations_h, flags_h, samples, history, window_h, first_h, tcos_h, tsin_h, second_h, perm_h, out, onehot,
     stream, window, first, tcos, tsin, second, perm, filtered, lanes, full, messages,
-    sem, lead_sem, lead_send, send_sem, recv_sem, own_sem,
+    channels, stations, flags, where, place, sem, lead_sem, lead_send, send_sem, recv_sem, own_sem,
 ):
     st, tm, pol = lax.axis_index("st"), lax.axis_index("tm"), lax.axis_index("pol")
     z, y, w = st // 4, st % 4, tm * 2 + pol
@@ -79,12 +79,12 @@
     moves = [
         (samples.at[rows], stream.at[:, pl.ds(lead, FRAMES * NFFT)]),
         (window_h, window), (first_h, first), (tcos_h, tcos), (tsin_h, tsin),
-        (second_h, second), (perm_h, perm),
+        (second_h, second), (perm_h, perm), (channels_h, channels), (stations_h, stations), (flags_h, flags),
     ]
     copies = [pltpu.make_async_copy(s, d, sem.at[i]) for i, (s, d) in enumerate(moves)]
     for c in copies:
         c.start()
-    before = pltpu.make_async_copy(history.at[rows], stream.at[:, pl.ds(0, lead)], sem.at[7])
+    before = pltpu.make_async_copy(history.at[rows], stream.at[:, pl.ds(0, lead)], sem.at[len(moves)])
     pl.when(tm == 0)(before.start)
 
     barrier = pltpu.get_barrier_semaphore()
@@ -125,6 +125,14 @@
 
         lax.fori_loop(0, 32, step, 0)
 
+    for c in copies[7:]:
+        c.wait()
+    f = channels[...] // FRAME_A
+    order = lax.broadcasted_iota(jnp.int32, (16, 128), 1) % 8
+    where[0:16] = f // 8 * 32 + channels[...] % FRAME_A
+    where[16:32] = (8 + order - f % 8) % 8 * 16
+    placing = pltpu.make_async_copy(where, place, sem.at[len(moves) + 1])
+    placing.start()
     row = lax.broadcasted_iota(jnp.int32, (ROWS, 128), 0) // 2
     keep = jnp.zeros((ROWS, 128), F32)
     for i in range(ROWS // 2):
@@ -202,23 +210,30 @@
     slot = tm * 64 + st * 2 + pol
 
     def send(o, carry):
-        def one(j, a, b, c):
+        def gather(j, a, b, c):
             peer = a * 8 + b * 2 + c
             acc = None
             for i in range(8):
-                ch = channels[peer * 8 + i]
-                v = full[ch // 256 * 32 + ch % 32]
-                v = pltpu.roll(v, (8 + i - ch // 32 % 8) % 8 * 16, 1)
+                at, col = peer // 16, peer % 16 * 8 + i
+                v = pltpu.roll(full[place[at, col]], place[16 + at, col], 1)
                 acc = v if acc is None else jnp.where(lane == i, v, acc)
-            messages[peer] = acc.astype(BF16)
+            return acc.astype(BF16)
+
+        def one(j, a, b, c):
+            peer = a * 8 + b * 2 + c
             when_other(j, o, pltpu.make_async_remote_copy(
                 messages.at[peer], out.at[slot], send_sem, recv_sem,
                 device_id=(a, b, c), device_id_type=MESH,
             ).start)
 
+        made = []
+        each(lambda *at: made.append((at, gather(*at))), o)
+        for (j, a, b, c), block in made:
+            messages[a * 8 + b * 2 + c] = block
         each(one, o)
         return carry
 
+    placing.wait()
     lax.fori_loop(0, 32, send, 0)
     own = pltpu.make_async_copy(messages.at[st * 8 + w], out.at[slot], own_sem)
     own.start()
@@ -248,13 +263,12 @@
 
 def spectra(channels, stations, flags, samples, history):
     consts = [jnp.asarray(c) for c in constants()]
-    anyspec = pl.BlockSpec(memory_space=pl.ANY)
+    hbm = pl.BlockSpec(memory_space=pltpu.HBM)
     vmem = pl.BlockSpec(memory_space=pltpu.VMEM)
-    smem = pl.BlockSpec(memory_space=pltpu.SMEM)
     return pl.pallas_call(
         spectra_kernel,
         out_shape=[jax.ShapeDtypeStruct((PEERS, ROWS, 128), BF16), jax.ShapeDtypeStruct((512, 512), BF16)],
-        in_specs=[smem] * 3 + [anyspec] * 8,
+        in_specs=[hbm] * 11,
         out_specs=[vmem, vmem],
         scratch_shapes=[
             pltpu.VMEM((ROWS, (FRAMES + LEAD) * NFFT), BF16),
@@ -268,12 +282,17 @@
             pltpu.VMEM((256, 1024), BF16),
             pltpu.VMEM((256, ROWS, 128), F32),
             pltpu.VMEM((PEERS, ROWS, 128), BF16),
-            pltpu.SemaphoreType.DMA((8,)),
+            pltpu.VMEM((16, 128), jnp.int32),
+            pltpu.SMEM((256,), jnp.int32),
+            pltpu.SMEM((256,), jnp.int32),
+            pltpu.VMEM((32, 128), jnp.int32),
+            pltpu.SMEM((32, 128), jnp.int32),
+            pltpu.SemaphoreType.DMA((12,)),
             pltpu.SemaphoreType.DMA((2,)),
             pltpu.SemaphoreType.DMA((2,)),
         ] + [pltpu.SemaphoreType.DMA] * 3,
         compiler_params=pltpu.CompilerParams(
-            vmem_limit_bytes=40 << 20, collective_id=0, has_side_effects=True
+            vmem_limit_bytes=60 << 20, collective_id=0, has_side_effects=True
         ),
         name="spectra",
     )(channels, stations, flags, samples, history, *consts)
@@ -328,7 +347,7 @@
 
 
 def body(samples, history, station_order, channel_order, flagged):
-    turned, onehot = spectra(channel_order, station_order, flagged, samples, history)
+    turned, onehot = spectra(channel_order.reshape(16, 128), station_order, flagged, samples, history)
     return correlate(turned.reshape(4, 512, 128), onehot)
 
 

time: 82.4 us -> 51.2 us (0.62)
  Pallas kernels: 71 us -> 48.9 us
  local copies, waits for them, and re-layouts: 11 us -> 2.08 us
    pallas_call x1, Pallas kernels: 64.7 us -> 42.6 us  [spectra(): pl.pallas_call(spectra_kernel, out_shape=[jax.ShapeDtypeStruct((PEERS, RO...]
    unnamed x22 -> x4, local copies, waits for them, and re-layouts: 11 us -> 2.08 us
where the time goes in v3:
time: 51.2 us; the launch traced here: 51 us
  Pallas kernels  48.9 us (96%)
  local copies, waits for them, and re-layouts  2.08 us (4%)
    pallas_call x1, Pallas kernels, spectra(): pl.pallas_call(spectra_kernel, out_shape=[jax.ShapeDtypeStruct((PEERS, RO...  42.6 us
    pallas_call x1, Pallas kernels, correlate(): pl.pallas_call(correlate_kernel, out_shape=jax.ShapeDtypeStruct((8, 512,...  6.3 us
    unnamed x4, local copies, waits for them, and re-layouts  2.08 us

profile of v3, /device:TPU:2, one launch (start us, length us, event | category | flops | bytes accessed | tf_op | source)
XLA Modules:
  0.0 51.0 jit_solution(7787837092838134186)
XLA Ops:
  0.0 42.6 %spectra.1 = (bf16[256,8,128]{2,1,0:T(8,128)(2,1)}, bf16[512,512]{1,0:T(8,128)(2,1)}) custom-call(s32[16,128]{1,0:T(8,128)} %bitcast.3, s32[256]{0:T(256)} %stations_h.1, s32[256]{0:T(256)} %flags_h.1, bf16[16,65536]{1,0:T(8,128)(2,1)} %samples.1, bf16[16,24576]{1,0:T(8,128)(2,1)} %history.1, f32[4,8192]{1,0:T(4,128)} %constant.12.clone.window_h, ...), custom_call_target="tpu_custom_call" | custom-call | tf_op jit(solution)/shard_map/spectra/pallas_call | solution.py:268
  42.7 0.0 copy-start
  42.7 1.0 %copy-done = bf16[256,8,128]{2,1,0:T(8,128)(2,1)S(1)} copy-done((bf16[256,8,128]{2,1,0:T(8,128)(2,1)S(1)}, bf16[256,8,128]{2,1,0:T(8,128)(2,1)}, u32[]{:S(2)}) %copy-start) | copy-done | bytes 524312
  43.7 0.0 copy-start.1
  43.7 1.0 %copy-done.1 = bf16[512,512]{1,0:T(8,128)(2,1)S(1)} copy-done((bf16[512,512]{1,0:T(8,128)(2,1)S(1)}, bf16[512,512]{1,0:T(8,128)(2,1)}, u32[]{:S(2)}) %copy-start.1) | copy-done | bytes 524312
  44.7 6.3 %correlate.1 = f32[8,512,512]{2,1,0:T(8,128)} custom-call(bf16[4,512,128]{2,1,0:T(8,128)(2,1)S(1)} %bitcast.2, bf16[512,512]{1,0:T(8,128)(2,1)S(1)} %copy-done.1), custom_call_target="tpu_custom_call" | custom-call | tf_op jit(solution)/shard_map/correlate/pallas_call | solution.py:334
Async XLA Ops:
  42.7 1.0 %copy-start = (bf16[256,8,128]{2,1,0:T(8,128)(2,1)S(1)}, bf16[256,8,128]{2,1,0:T(8,128)(2,1)}, u32[]{:S(2)}) copy-start(bf16[256,8,128]{2,1,0:T(8,128)(2,1)} %get-tuple-element.7) | copy-start | bytes 1572868
  43.7 1.0 %copy-start.1 = (bf16[512,512]{1,0:T(8,128)(2,1)S(1)}, bf16[512,512]{1,0:T(8,128)(2,1)}, u32[]{:S(2)}) copy-start(bf16[512,512]{1,0:T(8,128)(2,1)} %get-tuple-element.8.onehot) | copy-start | bytes 1572868

commit v4 on v3

--- a/solution.py
+++ b/solution.py
@@ -20,8 +20,10 @@
 ROWS = 8
 FRAMES = 8
 PEERS = 256
+UNROLL = True
+GROUP = 4
 MESH = pl.DeviceIdType.MESH
-Z_OFFSETS = (1, 7, 2, 6, 3, 5, 4, 0)
+Z_OFFSETS = (4, 3, 5, 2, 6, 1, 7, 0)
 BF16 = jnp.bfloat16
 F32 = jnp.float32
 
@@ -46,7 +48,7 @@
     angle = (b[:, None] * f[None, :] % FRAME_B) * (2.0 * math.pi / FRAME_B)
     cos = (np.cos(angle) / math.sqrt(FRAME_B)).astype(bf)
     sin = (-np.sin(angle) / math.sqrt(FRAME_B)).astype(bf)
-    second = np.concatenate([np.concatenate([cos, sin], 1), np.concatenate([-sin, cos], 1)], 0)
+    second = np.concatenate([np.concatenate([cos, sin, sin, cos], 1), np.concatenate([-sin, cos, cos, -sin], 1)], 0)
     t, p, f = np.meshgrid(np.arange(FRAMES), np.arange(2), np.arange(64), indexing="ij")
     perm = np.zeros((1024, 1024), np.float32)
     perm[(t * 128 + p * 64 + f).ravel(), (f * 16 + p * 8 + t).ravel()] = 1
@@ -55,8 +57,8 @@
 
 def spectra_kernel(
     channels_h, stations_h, flags_h, samples, history, window_h, first_h, tcos_h, tsin_h, second_h, perm_h, out, onehot,
-    stream, window, first, tcos, tsin, second, perm, filtered, lanes, full, messages,
-    channels, stations, flags, where, place, sem, lead_sem, lead_send, send_sem, recv_sem, own_sem,
+    stream, window, first, tcos, tsin, second, perm, filtered, lanes, chosen, messages,
+    channels, stations, flags, sem, lead_sem, lead_send, send_sem, recv_sem, own_sem,
 ):
     st, tm, pol = lax.axis_index("st"), lax.axis_index("tm"), lax.axis_index("pol")
     z, y, w = st // 4, st % 4, tm * 2 + pol
@@ -127,18 +129,12 @@
 
     for c in copies[7:]:
         c.wait()
-    f = channels[...] // FRAME_A
-    order = lax.broadcasted_iota(jnp.int32, (16, 128), 1) % 8
-    where[0:16] = f // 8 * 32 + channels[...] % FRAME_A
-    where[16:32] = (8 + order - f % 8) % 8 * 16
-    placing = pltpu.make_async_copy(where, place, sem.at[len(moves) + 1])
-    placing.start()
     row = lax.broadcasted_iota(jnp.int32, (ROWS, 128), 0) // 2
     keep = jnp.zeros((ROWS, 128), F32)
     for i in range(ROWS // 2):
         flag = 1 - flags[stations[st * 8 + pol * 4 + i]]
         keep = jnp.where(row == i, flag.astype(F32), keep)
-    keep = jnp.tile(keep, (FRAME_A, 1))
+    low = lax.broadcasted_iota(jnp.int32, (ROWS, 128), 1) < 64
 
     def frame(t, carry):
         seg = jnp.dot(first[...], filtered[t], preferred_element_type=F32)
@@ -162,14 +158,20 @@
         tw = jnp.concatenate(
             [jnp.concatenate(res, axis=0).astype(BF16), jnp.concatenate(ims, axis=0).astype(BF16)], axis=1
         )
-        spec = jnp.dot(tw, second[...], preferred_element_type=F32) * keep
-        lanes[:, pl.ds(pl.multiple_of(t * 128, 128), 128)] = spec.astype(BF16)
+        spec = jnp.dot(tw, second[...], preferred_element_type=F32)
+        for e in range(0, FRAME_A, 2):
+            one, two = (spec[i * ROWS : (i + 1) * ROWS] for i in (e, e + 1))
+            both = [
+                jnp.where(low, one[:, :128], two[:, 128:]) * keep,
+                jnp.where(low, one[:, 128:], two[:, :128]) * keep,
+            ]
+            lanes[pl.ds(pl.multiple_of(t * 16, 16), 16), e * 64 : e * 64 + 128] = jnp.concatenate(both, axis=0).astype(BF16)
         return carry
 
     taps(LEAD, FRAMES)
     for c in copies[2:6]:
         c.wait()
-    lax.fori_loop(LEAD, FRAMES, frame, 0)
+    lax.fori_loop(LEAD, FRAMES, frame, 0, unroll=UNROLL)
 
     pl.semaphore_wait(barrier, PEERS - 1)
 
@@ -191,6 +193,20 @@
         for c in leads:
             c.start()
 
+    order = channels[...]
+    channels[...] = order % FRAME_A * 64 + order // FRAME_A
+    at = lax.broadcasted_iota(jnp.int32, (256, 128), 0)
+
+    def choose(i, carry):
+        for h in range(2):
+            wanted = jnp.broadcast_to(channels[pl.ds(2 * i + h, 1), :], (256, 128))
+            for k in range(8):
+                block = jnp.where(at == wanted - 256 * k, 1.0, 0.0).astype(BF16)
+                chosen[i, k * 256 : (k + 1) * 256, h * 128 : (h + 1) * 128] = block
+        return carry
+
+    lax.fori_loop(0, 8, choose, 0)
+
     @pl.when(tm != 0)
     def _():
         for c in leads:
@@ -198,43 +214,47 @@
 
     pl.when(tm == 0)(before.wait)
     taps(0, LEAD)
-    lax.fori_loop(0, LEAD, frame, 0)
+    lax.fori_loop(0, LEAD, frame, 0, unroll=UNROLL)
     copies[6].wait()
-    for q in range(4):
-        turned = jnp.dot(lanes[...], perm[:, q * 256 : (q + 1) * 256], preferred_element_type=F32)
+    slot = tm * 64 + st * 2 + pol
+
+    def blocks(s):
+        picked = jnp.dot(lanes[...], chosen[s], preferred_element_type=F32)
+        rows = []
         for h in range(2):
-            block = 2 * q + h
-            full[block * 32 : (block + 1) * 32] = turned[:, h * 128 : (h + 1) * 128].reshape(32, ROWS, 128)
-
-    lane = lax.broadcasted_iota(jnp.int32, (ROWS, 128), 1) // 16
-    slot = tm * 64 + st * 2 + pol
-
-    def send(o, carry):
-        def gather(j, a, b, c):
-            peer = a * 8 + b * 2 + c
-            acc = None
-            for i in range(8):
-                at, col = peer // 16, peer % 16 * 8 + i
-                v = pltpu.roll(full[place[at, col]], place[16 + at, col], 1)
-                acc = v if acc is None else jnp.where(lane == i, v, acc)
-            return acc.astype(BF16)
-
-        def one(j, a, b, c):
-            peer = a * 8 + b * 2 + c
-            when_other(j, o, pltpu.make_async_remote_copy(
-                messages.at[peer], out.at[slot], send_sem, recv_sem,
-                device_id=(a, b, c), device_id_type=MESH,
-            ).start)
-
-        made = []
-        each(lambda *at: made.append((at, gather(*at))), o)
-        for (j, a, b, c), block in made:
-            messages[a * 8 + b * 2 + c] = block
-        each(one, o)
-        return carry
-
-    placing.wait()
-    lax.fori_loop(0, 32, send, 0)
+            first_half, second_half = [], []
+            for t in range(FRAMES):
+                re, im = (picked[t * 16 + p * 8 : t * 16 + p * 8 + 8, h * 128 : (h + 1) * 128] for p in range(2))
+                first_half.append(jnp.where(low, re, pltpu.roll(im, 64, 1)))
+                second_half.append(jnp.where(low, pltpu.roll(re, 64, 1), im))
+            rows += [jnp.concatenate(first_half, axis=1), jnp.concatenate(second_half, axis=1)]
+        return jnp.concatenate(rows, axis=0)
+
+    def send(i, carry):
+        near = [zs[GROUP * i + g] for g in range(GROUP)] if isinstance(i, int) else None
+        stacked = jnp.concatenate([blocks(s) for s in near], axis=0).astype(BF16)
+        for q in range(4):
+            turned = jnp.dot(stacked, perm[:, q * 256 : (q + 1) * 256], preferred_element_type=F32).astype(BF16)
+            for g, s in enumerate(near):
+                for b in range(4):
+                    for h in range(2):
+                        messages[s * 32 + b * 8 + 2 * q + h] = turned[g * 32 + b * 8 : g * 32 + b * 8 + 8, h * 128 : (h + 1) * 128]
+
+        def ship(o, carry):
+            yy, ww = (y + o % 4) % 4, (w + o // 4) % 8
+            for g, s in enumerate(near):
+                a = s * 4 + yy
+                when_other(GROUP * i + g, o, pltpu.make_async_remote_copy(
+                    messages.at[a * 8 + ww], out.at[slot], send_sem, recv_sem,
+                    device_id=(a, ww // 2, ww % 2), device_id_type=MESH,
+                ).start)
+            return carry
+
+        lax.fori_loop(0, 32, ship, 0)
+        return carry
+
+    for i in range(8 // GROUP):
+        send(i, 0)
     own = pltpu.make_async_copy(messages.at[st * 8 + w], out.at[slot], own_sem)
     own.start()
 
@@ -276,17 +296,15 @@
             pltpu.VMEM((256, 256), BF16),
             pltpu.VMEM((256, 256), F32),
             pltpu.VMEM((256, 256), F32),
-            pltpu.VMEM((512, 128), BF16),
+            pltpu.VMEM((512, 256), BF16),
             pltpu.VMEM((1024, 1024), BF16),
             pltpu.VMEM((FRAMES, 256, 256), BF16),
-            pltpu.VMEM((256, 1024), BF16),
-            pltpu.VMEM((256, ROWS, 128), F32),
+            pltpu.VMEM((128, CH), BF16),
+            pltpu.VMEM((8, CH, 256), BF16),
             pltpu.VMEM((PEERS, ROWS, 128), BF16),
             pltpu.VMEM((16, 128), jnp.int32),
             pltpu.SMEM((256,), jnp.int32),
             pltpu.SMEM((256,), jnp.int32),
-            pltpu.VMEM((32, 128), jnp.int32),
-            pltpu.SMEM((32, 128), jnp.int32),
             pltpu.SemaphoreType.DMA((12,)),
             pltpu.SemaphoreType.DMA((2,)),
             pltpu.SemaphoreType.DMA((2,)),
@@ -298,50 +316,71 @@
     )(channels, stations, flags, samples, history, *consts)
 
 
-def correlate_kernel(turned, onehot, out, parts, swapped):
-    slot = pl.program_id(0)
-
-    @pl.when(slot == 0)
-    def _():
-        for tm in range(4):
-            got = lax.dot_general(
-                turned[tm], onehot[...], (((0,), (0,)), ((), ())), preferred_element_type=F32
+def correlate_kernel(turned_h, onehot_h, out, turned, onehot, parts, swapped, blocks, in_sem, out_sem):
+    loads = [pltpu.make_async_copy(onehot_h, onehot, in_sem.at[4])] + [
+        pltpu.make_async_copy(turned_h.at[tm], turned.at[tm], in_sem.at[tm]) for tm in range(4)
+    ]
+    for c in loads:
+        c.start()
+    loads[0].wait()
+    for tm in range(4):
+        loads[tm + 1].wait()
+        got = lax.dot_general(
+            turned[tm], onehot[...], (((0,), (0,)), ((), ())), preferred_element_type=F32
+        )
+        for s in range(8):
+            re, im = got[16 * s : 16 * s + 8], got[16 * s + 8 : 16 * s + 16]
+            parts[s, 16 * tm : 16 * tm + 16] = jnp.concatenate([re, im], axis=0).astype(BF16)
+            swapped[s, 16 * tm : 16 * tm + 16] = jnp.concatenate([-im, re], axis=0).astype(BF16)
+
+    upper = lax.broadcasted_iota(jnp.int32, (256, 256), 0) <= lax.broadcasted_iota(jnp.int32, (256, 256), 1)
+
+    def write(slot, i):
+        rows = pl.ds(i * 256, 256)
+        return pltpu.make_async_copy(blocks.at[slot, rows], out.at[slot, rows], out_sem.at[slot, i])
+
+    def step(slot, carry):
+        part, swap = parts[slot], swapped[slot]
+
+        def product(i, right, j):
+            return lax.dot_general(
+                part[:, i * 256 : i * 256 + 256], right[:, j * 256 : j * 256 + 256],
+                (((0,), (0,)), ((), ())), preferred_element_type=F32,
             )
-            for s in range(8):
-                re, im = got[16 * s : 16 * s + 8], got[16 * s + 8 : 16 * s + 16]
-                parts[s, 16 * tm : 16 * tm + 16] = jnp.concatenate([re, im], axis=0).astype(BF16)
-                swapped[s, 16 * tm : 16 * tm + 16] = jnp.concatenate([-im, re], axis=0).astype(BF16)
-
-    part, swap = parts[slot], swapped[slot]
-
-    def product(i, right, j):
-        return lax.dot_general(
-            part[:, i * 256 : i * 256 + 256], right[:, j * 256 : j * 256 + 256],
-            (((0,), (0,)), ((), ())), preferred_element_type=F32,
-        )
-
-    upper = lax.broadcasted_iota(jnp.int32, (256, 256), 0) <= lax.broadcasted_iota(jnp.int32, (256, 256), 1)
-    for i in range(2):
-        for j in range(2):
-            if i == j:
-                block = jnp.where(upper, product(i, part, j), product(i, swap, j))
-            else:
-                block = product(i, part if i < j else swap, j)
-            out[0, i * 256 : i * 256 + 256, j * 256 : j * 256 + 256] = block * (1.0 / 32)
+
+        for i in range(2):
+            for j in range(2):
+                if i == j:
+                    block = jnp.where(upper, product(i, part, j), product(i, swap, j))
+                else:
+                    block = product(i, part if i < j else swap, j)
+                blocks[slot, i * 256 : i * 256 + 256, j * 256 : j * 256 + 256] = block * (1.0 / 32)
+            write(slot, i).start()
+        return carry
+
+    lax.fori_loop(0, 8, step, 0, unroll=4)
+    for slot in range(8):
+        for i in range(2):
+            write(slot, i).wait()
 
 
 def correlate(turned, onehot):
+    hbm = pl.BlockSpec(memory_space=pltpu.HBM)
     return pl.pallas_call(
         correlate_kernel,
         out_shape=jax.ShapeDtypeStruct((8, 512, 512), F32),
-        grid=(8,),
-        in_specs=[
-            pl.BlockSpec((4, 512, 128), lambda s: (0, 0, 0)),
-            pl.BlockSpec((512, 512), lambda s: (0, 0)),
+        in_specs=[hbm, hbm],
+        out_specs=hbm,
+        scratch_shapes=[
+            pltpu.VMEM((4, 512, 128), BF16),
+            pltpu.VMEM((512, 512), BF16),
+            pltpu.VMEM((8, 64, 512), BF16),
+            pltpu.VMEM((8, 64, 512), BF16),
+            pltpu.VMEM((8, 512, 512), F32),
+            pltpu.SemaphoreType.DMA((5,)),
+            pltpu.SemaphoreType.DMA((8, 2)),
         ],
-        out_specs=pl.BlockSpec((1, 512, 512), lambda s: (s, 0, 0)),
-        scratch_shapes=[pltpu.VMEM((8, 64, 512), BF16), pltpu.VMEM((8, 64, 512), BF16)],
-        compiler_params=pltpu.CompilerParams(vmem_limit_bytes=24 << 20),
+        compiler_params=pltpu.CompilerParams(vmem_limit_bytes=60 << 20),
         name="correlate",
     )(turned, onehot)
 

time: 51.2 us -> 42.9 us (0.84)
  the two profiles are of different devices: /device:TPU:2 before, /device:TPU:1 now
where the time goes in v4:
time: 42.9 us; the launch traced here: 42.8 us
  Pallas kernels  42.8 us (100%)
    pallas_call x1, Pallas kernels, spectra(): pl.pallas_call(spectra_kernel, out_shape=[jax.ShapeDtypeStruct((PEERS, RO...  36.9 us
    pallas_call x1, Pallas kernels, correlate(): pl.pallas_call(correlate_kernel, out_shape=jax.ShapeDtypeStruct((8, 512,...  5.87 us

profile of v4, /device:TPU:1, one launch (start us, length us, event | category | flops | bytes accessed | tf_op | source)
XLA Modules:
  0.0 42.8 jit_solution(6738673921444770642)
XLA Ops:
  0.0 36.9 %spectra.1 = (bf16[256,8,128]{2,1,0:T(8,128)(2,1)}, bf16[512,512]{1,0:T(8,128)(2,1)}) custom-call(s32[16,128]{1,0:T(8,128)} %bitcast.3, s32[256]{0:T(256)} %stations_h.1, s32[256]{0:T(256)} %flags_h.1, bf16[16,65536]{1,0:T(8,128)(2,1)} %samples.1, bf16[16,24576]{1,0:T(8,128)(2,1)} %history.1, f32[4,8192]{1,0:T(4,128)} %constant.12.clone.window_h, ...), custom_call_target="tpu_custom_call" | custom-call | tf_op jit(solution)/shard_map/spectra/pallas_call | solution.py:288
  36.9 5.9 %correlate.1 = f32[8,512,512]{2,1,0:T(8,128)} custom-call(bf16[4,512,128]{2,1,0:T(8,128)(2,1)} %bitcast.2, bf16[512,512]{1,0:T(8,128)(2,1)} %get-tuple-element.8.onehot_h), custom_call_target="tpu_custom_call" | custom-call | tf_op jit(solution)/shard_map/correlate/pallas_call | solution.py:369

commit v5 on v4

--- a/solution.py
+++ b/solution.py
@@ -100,7 +100,7 @@
         each(signal, o)
         return carry
 
-    lax.fori_loop(0, 32, greet, 0)
+    lax.fori_loop(0, 32, greet, 0, unroll=4)
     for c in copies[:2]:
         c.wait()
 
@@ -250,7 +250,7 @@
                 ).start)
             return carry
 
-        lax.fori_loop(0, 32, ship, 0)
+        lax.fori_loop(0, 32, ship, 0, unroll=4)
         return carry
 
     for i in range(8 // GROUP):
@@ -318,16 +318,18 @@
 
 def correlate_kernel(turned_h, onehot_h, out, turned, onehot, parts, swapped, blocks, in_sem, out_sem):
     loads = [pltpu.make_async_copy(onehot_h, onehot, in_sem.at[4])] + [
-        pltpu.make_async_copy(turned_h.at[tm], turned.at[tm], in_sem.at[tm]) for tm in range(4)
+        pltpu.make_async_copy(turned_h.at[tm], turned.at[:, pl.ds(tm * 128, 128)], in_sem.at[tm]) for tm in range(4)
     ]
     for c in loads:
         c.start()
     loads[0].wait()
+    for c in loads[1:]:
+        c.wait()
+    everything = lax.dot_general(
+        turned[...], onehot[...], (((0,), (0,)), ((), ())), preferred_element_type=F32
+    )
     for tm in range(4):
-        loads[tm + 1].wait()
-        got = lax.dot_general(
-            turned[tm], onehot[...], (((0,), (0,)), ((), ())), preferred_element_type=F32
-        )
+        got = everything[tm * 128 : (tm + 1) * 128]
         for s in range(8):
             re, im = got[16 * s : 16 * s + 8], got[16 * s + 8 : 16 * s + 16]
             parts[s, 16 * tm : 16 * tm + 16] = jnp.concatenate([re, im], axis=0).astype(BF16)
@@ -372,7 +374,7 @@
         in_specs=[hbm, hbm],
         out_specs=hbm,
         scratch_shapes=[
-            pltpu.VMEM((4, 512, 128), BF16),
+            pltpu.VMEM((512, 512), BF16),
             pltpu.VMEM((512, 512), BF16),
             pltpu.VMEM((8, 64, 512), BF16),
             pltpu.VMEM((8, 64, 512), BF16),

time: 42.9 us -> 41.8 us (0.974)
  Pallas kernels: 42.8 us -> 41.7 us
    pallas_call x1, Pallas kernels: 36.9 us -> 36.3 us  [spectra(): pl.pallas_call(spectra_kernel, out_shape=[jax.ShapeDtypeStruct((PEERS, RO...]
    pallas_call x1, Pallas kernels: 5.87 us -> 5.43 us  [correlate(): pl.pallas_call(correlate_kernel, out_shape=jax.ShapeDtypeStruct((8, 512,...]
where the time goes in v5:
time: 41.8 us; the launch traced here: 41.7 us
  Pallas kernels  41.7 us (100%)
    pallas_call x1, Pallas kernels, spectra(): pl.pallas_call(spectra_kernel, out_shape=[jax.ShapeDtypeStruct((PEERS, RO...  36.3 us
    pallas_call x1, Pallas kernels, correlate(): pl.pallas_call(correlate_kernel, out_shape=jax.ShapeDtypeStruct((8, 512,...  5.43 us

profile of v5, /device:TPU:1, one launch (start us, length us, event | category | flops | bytes accessed | tf_op | source)
XLA Modules:
  0.0 41.7 jit_solution(5372299110331840627)
XLA Ops:
  0.0 36.3 %spectra.1 = (bf16[256,8,128]{2,1,0:T(8,128)(2,1)}, bf16[512,512]{1,0:T(8,128)(2,1)}) custom-call(s32[16,128]{1,0:T(8,128)} %bitcast.3, s32[256]{0:T(256)} %stations_h.1, s32[256]{0:T(256)} %flags_h.1, bf16[16,65536]{1,0:T(8,128)(2,1)} %samples.1, bf16[16,24576]{1,0:T(8,128)(2,1)} %history.1, f32[4,8192]{1,0:T(4,128)} %constant.12.clone.window_h, ...), custom_call_target="tpu_custom_call" | custom-call | tf_op jit(solution)/shard_map/spectra/pallas_call | solution.py:288
  36.3 5.4 %correlate.1 = f32[8,512,512]{2,1,0:T(8,128)} custom-call(bf16[4,512,128]{2,1,0:T(8,128)(2,1)} %bitcast.2, bf16[512,512]{1,0:T(8,128)(2,1)} %get-tuple-element.8.onehot_h), custom_call_target="tpu_custom_call" | custom-call | tf_op jit(solution)/shard_map/correlate/pallas_call | solution.py:371
